TPU v7x, 32 devices: a whole 2x2x4 slice. The times are simulated.
32 devices in a mesh: dp: 16 (over z, y, x), tensor: 2 (over core).
Axes of the slice: x: 2, y: 2, z: 4, core: 2. Of those that a mesh axis runs over, the one named last changes fastest.
Arguments:
- frames: bfloat16 [2, 32, 512, 512], P(None, ('dp', 'tensor')), may hold values from -6 to 6
- lengths: int32 [2, 32], P(None, 'dp'), may hold values from 128 to 512, as said below
- ffn1_in: bfloat16 [512, 2048], P('dp', 'tensor'), may hold values from -0.25 to 0.25
- ffn1_out: bfloat16 [2048, 512], P('tensor', 'dp'), may hold values from -0.125 to 0.125
- ffn1_bias: bfloat16 [16, 128], P('tensor', 'dp'), may hold values from -3 to 3
- qkv_weight: bfloat16 [512, 3, 512], P('dp', None, 'tensor'), may hold values from -0.25 to 0.25
- pos_weight: bfloat16 [512, 512], P('dp', 'tensor'), may hold values from -0.25 to 0.25
- out_weight: bfloat16 [512, 512], P('tensor', 'dp'), may hold values from -1 to 1
- attn_bias: bfloat16 [4, 4, 128], P(None, 'tensor', 'dp'), may hold values from -3 to 3
- conv_in: bfloat16 [512, 2, 512], P('dp', None, 'tensor'), may hold values from -0.25 to 0.25
- conv_out: bfloat16 [512, 512], P('tensor', 'dp'), may hold values from -0.25 to 0.25
- conv_channel: bfloat16 [13, 4, 128], P(None, 'tensor', 'dp'), may hold values from -2 to 2
- ffn2_in: bfloat16 [512, 2048], P('dp', 'tensor'), may hold values from -0.25 to 0.25
- ffn2_out: bfloat16 [2048, 512], P('tensor', 'dp'), may hold values from -0.125 to 0.125
- ffn2_bias: bfloat16 [16, 128], P('tensor', 'dp'), may hold values from -3 to 3
- norm_params: bfloat16 [14, 512], P(None, ('dp', 'tensor')), may hold values from -1.2 to 1.4
- cotangent: bfloat16 [2, 32, 512, 512], P(None, ('dp', 'tensor')), may hold values from -6 to 6
Outputs:
- activations: bfloat16 [2, 32, 512, 512], P(None, ('dp', 'tensor'))
- frame_grad: bfloat16 [2, 32, 512, 512], P(None, ('dp', 'tensor'))
- ffn1_in_grad: float32 [512, 2048], P('dp', 'tensor')
- ffn1_out_grad: float32 [2048, 512], P('tensor', 'dp')
- ffn1_bias_grad: float32 [16, 128], P('tensor', 'dp')
- qkv_grad: float32 [512, 3, 512], P('dp', None, 'tensor')
- pos_grad: float32 [512, 512], P('dp', 'tensor')
- out_grad: float32 [512, 512], P('tensor', 'dp')
- attn_bias_grad: float32 [4, 4, 128], P(None, 'tensor', 'dp')
- conv_in_grad: float32 [512, 2, 512], P('dp', None, 'tensor')
- conv_out_grad: float32 [512, 512], P('tensor', 'dp')
- conv_channel_grad: float32 [13, 4, 128], P(None, 'tensor', 'dp')
- ffn2_in_grad: float32 [512, 2048], P('dp', 'tensor')
- ffn2_out_grad: float32 [2048, 512], P('tensor', 'dp')
- ffn2_bias_grad: float32 [16, 128], P('tensor', 'dp')
- norm_grad: float32 [14, 512], P(None, ('dp', 'tensor'))
Inputs may be any that keep to these rules, and one draw needn't show every extreme that they name: `lengths`: the last utterance of every micro-batch has 512 frames.
All inputs are finite; a program needn't handle non-finite values.
Results may differ from a plain program's by a relative error of at most 0.04.
Values may be sent and summed in bfloat16 or wider, within the bound.
A program may use at most 256 MiB of HBM per device.

v0:
```python
import math

import jax
import jax.numpy as jnp
from jax import lax
from jax.sharding import PartitionSpec as P

DK = 64


norm_eps = 1e-05
mask_fill = -1000000000.0


def position_table(length, width):
    offsets = (length - 1 - jnp.arange(2 * length - 1, dtype=jnp.int32)).astype(jnp.float32)
    freq_rates = jnp.exp(
        jnp.arange(0, width, 2, dtype=jnp.int32).astype(jnp.float32) * (-math.log(10000.0) / width)
    )
    angles = offsets[:, None] * freq_rates[None, :]
    return jnp.stack([jnp.sin(angles), jnp.cos(angles)], axis=-1).reshape(2 * length - 1, width)


def rel_shift(scores):
    leading = scores.shape[:-2]
    row_count = scores.shape[-2]
    col_count = scores.shape[-1]
    padded = jnp.pad(scores, [(0, 0)] * len(leading) + [(0, 0), (1, 0)])
    padded = padded.reshape(leading + (col_count + 1, row_count))
    return padded[..., 1:, :].reshape(leading + (row_count, col_count))[..., :row_count]


def swish_act(values):
    return values * jax.nn.sigmoid(values)


def swish_slope(values):
    sigma = jax.nn.sigmoid(values)
    return sigma + values * sigma * (1.0 - sigma)


def norm_forward(values, gain, shift):
    average = jnp.mean(values, axis=-1, keepdims=True)
    centered = values - average
    inv_std = lax.rsqrt(jnp.mean(centered * centered, axis=-1, keepdims=True) + norm_eps)
    scaled = centered * inv_std
    return (scaled * gain + shift, scaled, inv_std)


def norm_backward(upstream, scaled, inv_std, gain):
    grad_gain = jnp.sum(upstream * scaled, axis=(0, 1))
    grad_shift = jnp.sum(upstream, axis=(0, 1))
    grad_scaled = upstream * gain
    inner = (
        grad_scaled
        - jnp.mean(grad_scaled, axis=-1, keepdims=True)
        - scaled * jnp.mean(grad_scaled * scaled, axis=-1, keepdims=True)
    )
    return (inv_std * inner, grad_gain, grad_shift)


def depthwise(signal, taps_all):
    reach = (taps_all.shape[0] - 1) // 2
    length_now = signal.shape[1]
    padded = jnp.pad(signal, ((0, 0), (reach, reach), (0, 0)))
    summed = jnp.zeros_like(signal)
    for tap_idx in range(taps_all.shape[0]):
        summed = summed + taps_all[tap_idx] * padded[:, tap_idx : tap_idx + length_now]
    return summed


def depthwise_back(upstream, signal, taps_all):
    reach = (taps_all.shape[0] - 1) // 2
    length_now = upstream.shape[1]
    padded_grad = jnp.pad(upstream, ((0, 0), (reach, reach), (0, 0)))
    padded_sig = jnp.pad(signal, ((0, 0), (reach, reach), (0, 0)))
    grad_signal = jnp.zeros_like(signal)
    tap_grads = []
    for tap_idx in range(taps_all.shape[0]):
        begin = 2 * reach - tap_idx
        grad_signal = grad_signal + taps_all[tap_idx] * padded_grad[:, begin : begin + length_now]
        tap_grads.append(
            jnp.sum(upstream * padded_sig[:, tap_idx : tap_idx + length_now], axis=(0, 1))
        )
    return (grad_signal, jnp.stack(tap_grads))


def spread(values):
    return lax.all_gather(values, "tensor", axis=0, tiled=True)


def collect(values):
    return lax.psum_scatter(
        values.astype(jnp.bfloat16), "tensor", scatter_dimension=0, tiled=True
    ).astype(jnp.float32)


def spread_back(values):
    return lax.all_gather(values, "tensor", axis=0, tiled=True)


def collect_back(values):
    return lax.psum_scatter(
        values.astype(jnp.bfloat16), "tensor", scatter_dimension=0, tiled=True
    ).astype(jnp.float32)


def fetch_weights(
    ffn1_in,
    ffn1_out,
    ffn1_bias,
    qkv_weight,
    pos_weight,
    out_weight,
    attn_bias,
    conv_in,
    conv_out,
    conv_channel,
    ffn2_in,
    ffn2_out,
    ffn2_bias,
):
    return (
        lax.all_gather(ffn1_in, "dp", axis=0, tiled=True),
        lax.all_gather(ffn1_out, "dp", axis=1, tiled=True),
        lax.all_gather(ffn1_bias, "dp", axis=1, tiled=True),
        lax.all_gather(qkv_weight, "dp", axis=0, tiled=True),
        lax.all_gather(pos_weight, "dp", axis=0, tiled=True),
        lax.all_gather(out_weight, "dp", axis=1, tiled=True),
        lax.all_gather(attn_bias, "dp", axis=2, tiled=True),
        lax.all_gather(conv_in, "dp", axis=0, tiled=True),
        lax.all_gather(conv_out, "dp", axis=1, tiled=True),
        lax.all_gather(conv_channel, "dp", axis=2, tiled=True),
        lax.all_gather(ffn2_in, "dp", axis=0, tiled=True),
        lax.all_gather(ffn2_out, "dp", axis=1, tiled=True),
        lax.all_gather(ffn2_bias, "dp", axis=1, tiled=True),
    )


def reduce_grads(packed):
    return (
        lax.psum_scatter(packed[0], "dp", scatter_dimension=0, tiled=True),
        lax.psum_scatter(packed[1], "dp", scatter_dimension=1, tiled=True),
        lax.psum_scatter(packed[2], "dp", scatter_dimension=1, tiled=True),
        lax.psum_scatter(packed[3], "dp", scatter_dimension=0, tiled=True),
        lax.psum_scatter(packed[4], "dp", scatter_dimension=0, tiled=True),
        lax.psum_scatter(packed[5], "dp", scatter_dimension=1, tiled=True),
        lax.psum_scatter(packed[6], "dp", scatter_dimension=2, tiled=True),
        lax.psum_scatter(packed[7], "dp", scatter_dimension=0, tiled=True),
        lax.psum_scatter(packed[8], "dp", scatter_dimension=1, tiled=True),
        lax.psum_scatter(packed[9], "dp", scatter_dimension=2, tiled=True),
        lax.psum_scatter(packed[10], "dp", scatter_dimension=0, tiled=True),
        lax.psum_scatter(packed[11], "dp", scatter_dimension=1, tiled=True),
        lax.psum_scatter(packed[12], "dp", scatter_dimension=1, tiled=True),
    )


def arrange(gathered):
    (
        f1_in,
        f1_out,
        f1_bias,
        query_key_value_weight,
        pos_w,
        out_w,
        attn_vec,
        conv_w_in,
        conv_w_out,
        conv_vec,
        f2_in,
        f2_out,
        f2_bias,
    ) = gathered
    return {
        "ffn1": (f1_in, f1_out, f1_bias.astype(jnp.float32).reshape(-1)),
        "attn": (
            query_key_value_weight,
            pos_w,
            out_w,
            attn_vec.astype(jnp.float32).reshape(attn_vec.shape[0], -1),
        ),
        "conv": (
            conv_w_in,
            conv_w_out,
            conv_vec.astype(jnp.float32).reshape(conv_vec.shape[0], -1),
        ),
        "ffn2": (f2_in, f2_out, f2_bias.astype(jnp.float32).reshape(-1)),
    }


def ffn_forward(residual, gain, shift, out_bias, weights):
    input_weight, output_weight, input_bias = weights
    normed, scaled, inv_std = norm_forward(residual, gain, shift)
    normalized_input = spread(normed.astype(jnp.bfloat16))
    hidden_rows = (
        jnp.einsum(
            "yhu,ug->yhg", normalized_input, input_weight, preferred_element_type=jnp.float32
        )
        + input_bias
    )
    activated_rows = swish_act(hidden_rows).astype(jnp.bfloat16)
    partial_result = jnp.einsum(
        "xet,tu->xeu", activated_rows, output_weight, preferred_element_type=jnp.float32
    )
    return (
        collect(partial_result) + out_bias,
        (scaled, inv_std, normalized_input, hidden_rows, activated_rows),
    )


def ffn_backward(upstream, kept, gain, weights):
    scaled, inv_std, normalized_input, hidden_rows, activated_rows = kept
    input_weight, output_weight, input_bias = weights
    grad_round = upstream.astype(jnp.bfloat16)
    grad_out_bias = jnp.sum(grad_round.astype(jnp.float32), axis=(0, 1))
    combined_gradient = spread_back(grad_round)
    output_weight_gradient = jnp.einsum(
        "nzr,nzt->rt", activated_rows, combined_gradient, preferred_element_type=jnp.float32
    )
    activated_gradient = jnp.einsum(
        "vmz,az->vma", combined_gradient, output_weight, preferred_element_type=jnp.float32
    )
    hidden_gradient = (activated_gradient * swish_slope(hidden_rows)).astype(jnp.bfloat16)
    grad_b_in = jnp.sum(hidden_gradient.astype(jnp.float32), axis=(0, 1))
    grad_w_in = jnp.einsum(
        "pic,piv->cv", normalized_input, hidden_gradient, preferred_element_type=jnp.float32
    )
    grad_normed = collect_back(
        jnp.einsum("mtk,ak->mta", hidden_gradient, input_weight, preferred_element_type=jnp.float32)
    )
    grad_input, grad_gain, grad_shift = norm_backward(grad_normed, scaled, inv_std, gain)
    return (
        grad_input,
        (grad_w_in, output_weight_gradient, grad_b_in),
        (grad_gain, grad_shift, grad_out_bias),
    )


def attn_scores(query_u, query_v, key_rows, pos_rows, valid_full):
    content = jnp.einsum("sqhd,skhd->shqk", query_u, key_rows, preferred_element_type=jnp.float32)
    relative = rel_shift(
        jnp.einsum("sqhd,phd->shqp", query_v, pos_rows, preferred_element_type=jnp.float32)
    )
    scores = (content + relative) * (1.0 / math.sqrt(DK))
    return jnp.where(valid_full[:, None, None, :] > 0.5, scores, mask_fill)


def attn_forward(residual, gain, shift, out_bias, weights, valid_full, table):
    query_key_value_weight, pos_w, out_w, vectors = weights
    heads_here = query_key_value_weight.shape[-1] // DK
    normed, scaled, inv_std = norm_forward(residual, gain, shift)
    normalized_input = spread(normed.astype(jnp.bfloat16))
    seq_count, full_len = (normalized_input.shape[0], normalized_input.shape[1])
    head_shape = (seq_count, full_len, heads_here, DK)
    projected_rows = jnp.einsum(
        "xib,bwf->xiwf",
        normalized_input,
        query_key_value_weight,
        preferred_element_type=jnp.float32,
    )
    query = projected_rows[:, :, 0] + vectors[0]
    key_rows = projected_rows[:, :, 1].astype(jnp.bfloat16).reshape(head_shape)
    value_rows = (projected_rows[:, :, 2] + vectors[1]).astype(jnp.bfloat16).reshape(head_shape)
    query_u = (query + vectors[2]).astype(jnp.bfloat16).reshape(head_shape)
    query_v = (query + vectors[3]).astype(jnp.bfloat16).reshape(head_shape)
    pos_rows = (
        jnp.dot(table, pos_w, preferred_element_type=jnp.float32)
        .astype(jnp.bfloat16)
        .reshape(2 * full_len - 1, heads_here, DK)
    )
    masked = attn_scores(query_u, query_v, key_rows, pos_rows, valid_full)
    log_total = jax.nn.logsumexp(masked, axis=-1)
    attn_probs = jnp.exp(masked - log_total[..., None])
    mixed = jnp.einsum(
        "shqk,skhd->sqhd",
        attn_probs.astype(jnp.bfloat16),
        value_rows,
        preferred_element_type=jnp.float32,
    ).astype(jnp.bfloat16)
    mixed_flat = mixed.reshape(seq_count, full_len, -1)
    partial_result = jnp.einsum(
        "sqc,cd->sqd", mixed_flat, out_w, preferred_element_type=jnp.float32
    )
    kept = (
        scaled,
        inv_std,
        normalized_input,
        query_u,
        query_v,
        key_rows,
        value_rows,
        pos_rows,
        log_total,
        mixed_flat,
    )
    return (collect(partial_result) + out_bias, kept)


def attn_backward(upstream, kept, gain, weights, valid_full, table):
    (
        scaled,
        inv_std,
        normalized_input,
        query_u,
        query_v,
        key_rows,
        value_rows,
        pos_rows,
        log_total,
        mixed_flat,
    ) = kept
    query_key_value_weight, pos_w, out_w, vectors = weights
    seq_count, full_len, heads_here = (query_u.shape[0], query_u.shape[1], query_u.shape[2])
    score_scale = 1.0 / math.sqrt(DK)
    grad_round = upstream.astype(jnp.bfloat16)
    grad_out_bias = jnp.sum(grad_round.astype(jnp.float32), axis=(0, 1))
    combined_gradient = spread_back(grad_round)
    output_weight_gradient = jnp.einsum(
        "sqc,sqd->cd", mixed_flat, combined_gradient, preferred_element_type=jnp.float32
    )
    grad_mixed = jnp.einsum(
        "sqd,cd->sqc", combined_gradient, out_w, preferred_element_type=jnp.float32
    ).astype(jnp.bfloat16)
    grad_mixed = grad_mixed.reshape(seq_count, full_len, heads_here, DK)
    masked = attn_scores(query_u, query_v, key_rows, pos_rows, valid_full)
    attn_probs = jnp.exp(masked - log_total[..., None])
    grad_probs = jnp.einsum(
        "sqhd,skhd->shqk", grad_mixed, value_rows, preferred_element_type=jnp.float32
    )
    grad_scores = (
        attn_probs * (grad_probs - jnp.sum(grad_probs * attn_probs, axis=-1, keepdims=True))
    ).astype(jnp.bfloat16)
    grad_values = jnp.einsum(
        "shqk,sqhd->skhd",
        attn_probs.astype(jnp.bfloat16),
        grad_mixed,
        preferred_element_type=jnp.float32,
    ).astype(jnp.bfloat16)
    grad_qu = score_scale * jnp.einsum(
        "shqk,skhd->sqhd", grad_scores, key_rows, preferred_element_type=jnp.float32
    )
    grad_keys = (
        score_scale
        * jnp.einsum("shqk,sqhd->skhd", grad_scores, query_u, preferred_element_type=jnp.float32)
    ).astype(jnp.bfloat16)
    template = jnp.zeros((seq_count, heads_here, full_len, 2 * full_len - 1), jnp.float32)
    unused_out, shift_back = jax.vjp(rel_shift, template)
    grad_wide = shift_back(grad_scores.astype(jnp.float32))[0].astype(jnp.bfloat16)
    grad_qv = score_scale * jnp.einsum(
        "shqp,phd->sqhd", grad_wide, pos_rows, preferred_element_type=jnp.float32
    )
    grad_pos = (
        score_scale
        * jnp.einsum("shqp,sqhd->sphd", grad_wide, query_v, preferred_element_type=jnp.float32)
    ).astype(jnp.bfloat16)
    grad_pos_w = jnp.einsum(
        "pd,spc->dc",
        table,
        grad_pos.reshape(seq_count, 2 * full_len - 1, -1),
        preferred_element_type=jnp.float32,
    )
    grad_query = (grad_qu + grad_qv).astype(jnp.bfloat16).reshape(seq_count, full_len, -1)
    grad_keys = grad_keys.reshape(seq_count, full_len, -1)
    grad_values = grad_values.reshape(seq_count, full_len, -1)
    grad_vectors = jnp.stack(
        [
            jnp.sum(grad_query.astype(jnp.float32), axis=(0, 1)),
            jnp.sum(grad_values.astype(jnp.float32), axis=(0, 1)),
            jnp.sum(grad_qu, axis=(0, 1)).reshape(-1),
            jnp.sum(grad_qv, axis=(0, 1)).reshape(-1),
        ]
    )
    projected_gradient = jnp.stack([grad_query, grad_keys, grad_values], axis=2)
    grad_qkv = jnp.einsum(
        "fjp,fjmz->pmz", normalized_input, projected_gradient, preferred_element_type=jnp.float32
    )
    grad_normed = collect_back(
        jnp.einsum(
            "mthf,whf->mtw",
            projected_gradient,
            query_key_value_weight,
            preferred_element_type=jnp.float32,
        )
    )
    grad_input, grad_gain, grad_shift = norm_backward(grad_normed, scaled, inv_std, gain)
    return (
        grad_input,
        (grad_qkv, grad_pos_w, output_weight_gradient, grad_vectors),
        (grad_gain, grad_shift, grad_out_bias),
    )


def conv_forward(residual, gain, shift, out_bias, weights, valid_full):
    input_weight, output_weight, vectors = weights
    normed, scaled, inv_std = norm_forward(residual, gain, shift)
    normalized_input = spread(normed.astype(jnp.bfloat16))
    halves = (
        jnp.einsum(
            "xib,bwf->xiwf", normalized_input, input_weight, preferred_element_type=jnp.float32
        )
        + vectors[0:2]
    )
    gate_part = jax.nn.sigmoid(halves[:, :, 1])
    gated = halves[:, :, 0] * gate_part * valid_full[:, :, None]
    mixed = depthwise(gated, vectors[4:])
    mask_three = valid_full[:, :, None]
    stats = lax.psum(
        (
            jnp.sum(mixed * mask_three, axis=(0, 1)),
            jnp.sum(mixed * mixed * mask_three, axis=(0, 1)),
            jnp.sum(valid_full),
        ),
        "dp",
    )
    counted = stats[2]
    average = stats[0] / counted
    variance = stats[1] / counted - average * average
    bn_rstd = lax.rsqrt(variance + norm_eps)
    normal = (mixed - average) * bn_rstd
    before = normal * vectors[2] + vectors[3]
    activated_rows = swish_act(before).astype(jnp.bfloat16)
    partial_result = jnp.einsum(
        "ury,yb->urb", activated_rows, output_weight, preferred_element_type=jnp.float32
    )
    kept = (
        scaled,
        inv_std,
        normalized_input,
        halves,
        gate_part,
        gated,
        normal,
        before,
        activated_rows,
        bn_rstd,
        counted,
    )
    return (collect(partial_result) + out_bias, kept)


def conv_backward(upstream, kept, gain, weights, valid_full):
    (
        scaled,
        inv_std,
        normalized_input,
        halves,
        gate_part,
        gated,
        normal,
        before,
        activated_rows,
        bn_rstd,
        counted,
    ) = kept
    input_weight, output_weight, vectors = weights
    grad_round = upstream.astype(jnp.bfloat16)
    grad_out_bias = jnp.sum(grad_round.astype(jnp.float32), axis=(0, 1))
    combined_gradient = spread_back(grad_round)
    output_weight_gradient = jnp.einsum(
        "kua,kuf->af", activated_rows, combined_gradient, preferred_element_type=jnp.float32
    )
    activated_gradient = jnp.einsum(
        "eit,gt->eig", combined_gradient, output_weight, preferred_element_type=jnp.float32
    )
    grad_before = activated_gradient * swish_slope(before)
    grad_scale = jnp.sum(grad_before * normal, axis=(0, 1))
    grad_offset = jnp.sum(grad_before, axis=(0, 1))
    grad_normal = grad_before * vectors[2]
    back_sums = lax.psum(
        (jnp.sum(grad_normal, axis=(0, 1)), jnp.sum(grad_normal * normal, axis=(0, 1))), "dp"
    )
    mask_three = valid_full[:, :, None]
    grad_mixed = bn_rstd * (
        grad_normal - mask_three * (back_sums[0] + normal * back_sums[1]) / counted
    )
    grad_gated, grad_taps = depthwise_back(grad_mixed, gated, vectors[4:])
    grad_glu = grad_gated * mask_three
    grad_value = grad_glu * gate_part
    grad_gate = grad_glu * halves[:, :, 0] * gate_part * (1.0 - gate_part)
    split_gradient = jnp.stack([grad_value, grad_gate], axis=2).astype(jnp.bfloat16)
    grad_bias = jnp.sum(split_gradient.astype(jnp.float32), axis=(0, 1))
    grad_w_in = jnp.einsum(
        "fjp,fjmz->pmz", normalized_input, split_gradient, preferred_element_type=jnp.float32
    )
    grad_normed = collect_back(
        jnp.einsum(
            "mthf,whf->mtw", split_gradient, input_weight, preferred_element_type=jnp.float32
        )
    )
    grad_input, grad_gain, grad_shift = norm_backward(grad_normed, scaled, inv_std, gain)
    grad_vectors = jnp.concatenate(
        [grad_bias, grad_scale[None], grad_offset[None], grad_taps], axis=0
    )
    return (
        grad_input,
        (grad_w_in, output_weight_gradient, grad_vectors),
        (grad_gain, grad_shift, grad_out_bias),
    )


def local(
    frames,
    lengths,
    ffn1_in,
    ffn1_out,
    ffn1_bias,
    qkv_weight,
    pos_weight,
    out_weight,
    attn_bias,
    conv_in,
    conv_out,
    conv_channel,
    ffn2_in,
    ffn2_out,
    ffn2_bias,
    norm_params,
    cotangent,
):
    micro_count, seq_local, full_len, width = frames.shape
    seq_start = lax.axis_index("tensor") * seq_local
    norm_rows = lax.all_gather(norm_params, ("dp", "tensor"), axis=1, tiled=True).astype(
        jnp.float32
    )
    table = position_table(full_len, width).astype(jnp.bfloat16)
    positions = jnp.arange(full_len, dtype=jnp.int32)
    outputs_all = []
    inputs_all = []
    summed = None
    norm_total = jnp.zeros((norm_rows.shape[0], width), jnp.float32)
    for batch_idx in range(micro_count):
        weights_now = arrange(
            fetch_weights(
                ffn1_in,
                ffn1_out,
                ffn1_bias,
                qkv_weight,
                pos_weight,
                out_weight,
                attn_bias,
                conv_in,
                conv_out,
                conv_channel,
                ffn2_in,
                ffn2_out,
                ffn2_bias,
            )
        )
        valid_full = (positions[None, :] < lengths[batch_idx][:, None]).astype(jnp.float32)
        valid_local = lax.dynamic_slice_in_dim(valid_full, seq_start, seq_local, 0)
        residual_in = frames[batch_idx].astype(jnp.float32)
        branch_one, kept_one = ffn_forward(
            residual_in, norm_rows[0], norm_rows[1], norm_rows[2], weights_now["ffn1"]
        )
        residual_one = residual_in + 0.5 * branch_one
        branch_two, kept_two = attn_forward(
            residual_one,
            norm_rows[3],
            norm_rows[4],
            norm_rows[5],
            weights_now["attn"],
            valid_full,
            table,
        )
        residual_two = residual_one + branch_two
        branch_three, kept_three = conv_forward(
            residual_two, norm_rows[6], norm_rows[7], norm_rows[8], weights_now["conv"], valid_full
        )
        residual_three = residual_two + branch_three
        branch_four, kept_four = ffn_forward(
            residual_three, norm_rows[9], norm_rows[10], norm_rows[11], weights_now["ffn2"]
        )
        residual_four = residual_three + 0.5 * branch_four
        result, final_scaled, final_rstd = norm_forward(residual_four, norm_rows[12], norm_rows[13])
        outputs_all.append(result.astype(jnp.bfloat16))
        seed_grad = cotangent[batch_idx].astype(jnp.float32) * valid_local[:, :, None]
        grad_four, final_gain, final_shift = norm_backward(
            seed_grad, final_scaled, final_rstd, norm_rows[12]
        )
        delta_four, ffn2_grads, ffn2_norms = ffn_backward(
            0.5 * grad_four, kept_four, norm_rows[9], weights_now["ffn2"]
        )
        grad_three = grad_four + delta_four
        delta_three, conv_grads, conv_norms = conv_backward(
            grad_three, kept_three, norm_rows[6], weights_now["conv"], valid_full
        )
        grad_two = grad_three + delta_three
        delta_two, attn_grads, attn_norms = attn_backward(
            grad_two, kept_two, norm_rows[3], weights_now["attn"], valid_full, table
        )
        grad_one = grad_two + delta_two
        delta_one, ffn1_grads, ffn1_norms = ffn_backward(
            0.5 * grad_one, kept_one, norm_rows[0], weights_now["ffn1"]
        )
        inputs_all.append((grad_one + delta_one).astype(jnp.bfloat16))
        norm_total = norm_total + jnp.stack(
            ffn1_norms + attn_norms + conv_norms + ffn2_norms + (final_gain, final_shift)
        )
        packed = (
            ffn1_grads[0],
            ffn1_grads[1],
            ffn1_grads[2].reshape(ffn1_bias.shape[0], -1),
            attn_grads[0],
            attn_grads[1],
            attn_grads[2],
            attn_grads[3].reshape(attn_bias.shape[0], attn_bias.shape[1], -1),
            conv_grads[0],
            conv_grads[1],
            conv_grads[2].reshape(conv_channel.shape[0], conv_channel.shape[1], -1),
            ffn2_grads[0],
            ffn2_grads[1],
            ffn2_grads[2].reshape(ffn2_bias.shape[0], -1),
        )
        summed = packed if summed is None else jax.tree.map(jnp.add, summed, packed)
    summed = reduce_grads(summed)
    norm_grad = lax.psum_scatter(norm_total, ("dp", "tensor"), scatter_dimension=1, tiled=True)
    return (
        jnp.stack(outputs_all),
        jnp.stack(inputs_all),
        summed[0],
        summed[1],
        summed[2],
        summed[3],
        summed[4],
        summed[5],
        summed[6],
        summed[7],
        summed[8],
        summed[9],
        summed[10],
        summed[11],
        summed[12],
        norm_grad,
    )


def solution(mesh):
    in_specs = (
        P(None, ("dp", "tensor"), None, None),
        P(None, "dp"),
        P("dp", "tensor"),
        P("tensor", "dp"),
        P("tensor", "dp"),
        P("dp", None, "tensor"),
        P("dp", "tensor"),
        P("tensor", "dp"),
        P(None, "tensor", "dp"),
        P("dp", None, "tensor"),
        P("tensor", "dp"),
        P(None, "tensor", "dp"),
        P("dp", "tensor"),
        P("tensor", "dp"),
        P("tensor", "dp"),
        P(None, ("dp", "tensor")),
        P(None, ("dp", "tensor"), None, None),
    )
    out_specs = (
        P(None, ("dp", "tensor"), None, None),
        P(None, ("dp", "tensor"), None, None),
        P("dp", "tensor"),
        P("tensor", "dp"),
        P("tensor", "dp"),
        P("dp", None, "tensor"),
        P("dp", "tensor"),
        P("tensor", "dp"),
        P(None, "tensor", "dp"),
        P("dp", None, "tensor"),
        P("tensor", "dp"),
        P(None, "tensor", "dp"),
        P("dp", "tensor"),
        P("tensor", "dp"),
        P("tensor", "dp"),
        P(None, ("dp", "tensor")),
    )
    return jax.shard_map(local, mesh=mesh, in_specs=in_specs, out_specs=out_specs, check_vma=False)
```

profile of v0, /device:TPU:0, one launch (start us, length us, event | category | flops | bytes accessed | tf_op | source)
XLA Modules:
  0.0 2289.4 jit_solution(3134474103479814495)
XLA Ops:
  11.2 43.6 %all_gather.103 = bf16[14,512]{0,1:T(8,128)(2,1)S(1)} all-gather(bf16[14,16]{0,1:T(8,128)(2,1)S(1)} %copy.347), channel_id=1, replica_groups=mesh['dp'=16,'tensor'=2] {'dp','tensor'}, dimensions={1}, use_global_device_ids=true | all-gather | bytes 14784 | tf_op jit(solution)/shard_map/all_gather | solution.py:522
  61.0 35.7 %all_gather.106 = bf16[8,128]{0,1:T(8,128)(2,1)S(1)} all-gather(bf16[8,8]{0,1:T(8,128)(2,1)S(1)} %copy.348), channel_id=1, replica_groups=mesh['dp'=16,'tensor'=2] {'dp'}, dimensions={1}, use_global_device_ids=true | all-gather | bytes 2176 | tf_op jit(solution)/shard_map/all_gather | solution.py:126
  96.8 26.5 %all-gather.23.cloned.1.call-done = bf16[512,1024]{1,0:T(8,128)(2,1)} async-done(((bf16[32,1024]{1,0:T(8,128)(2,1)}), bf16[512,1024]{1,0:T(8,128)(2,1)}) %all-gather.23.cloned.1.call-update) | async-done | bytes 1048592 | tf_op jit(solution)/shard_map/all_gather | solution.py:124
  139.8 52.7 %all-gather.25.cloned.1.call-done = bf16[1024,512]{0,1:T(8,128)(2,1)} async-done(((bf16[1024,32]{0,1:T(8,128)(2,1)}), bf16[1024,512]{0,1:T(8,128)(2,1)}) %all-gather.25.cloned.1.call-update) | async-done | bytes 1048592 | tf_op jit(solution)/shard_map/all_gather | solution.py:125
  201.3 31.0 %multiply_sine_fusion = (bf16[1023,256,1]{0,2,1:T(2,128)(2,1)S(1)}, bf16[1023,256,1]{0,2,1:T(2,128)(2,1)S(1)}) fusion(f32[1023]{0:T(1024)S(1)} %subtract_convert_fusion, f32[256]{0:T(256)S(1)} %multiply_exponential_fusion), kind=kLoop, calls=%fused_computation.172 | loop fusion | flops 785664 | bytes 1052668 | tf_op jit(solution)/shard_map/sin | solution.py:21
  237.4 39.0 %all_gather.110 = bf16[4,2,128]{0,1,2:T(2,128)(2,1)S(1)} all-gather(bf16[4,2,8]{0,1,2:T(2,128)(2,1)S(1)} %copy.350), channel_id=1, replica_groups=mesh['dp'=16,'tensor'=2] {'dp'}, dimensions={2}, use_global_device_ids=true | all-gather | bytes 2176 | tf_op jit(solution)/shard_map/all_gather | solution.py:130
  282.0 36.9 %all_gather.111 = bf16[512,256]{1,0:T(8,128)(2,1)S(1)} all-gather(bf16[32,256]{1,0:T(8,128)(2,1)S(1)} %copy-done.109), channel_id=1, replica_groups=mesh['dp'=16,'tensor'=2] {'dp'}, dimensions={0}, use_global_device_ids=true | all-gather | bytes 278528 | tf_op jit(solution)/shard_map/all_gather | solution.py:128
  322.0 39.2 %all_gather.112 = bf16[256,512]{0,1:T(8,128)(2,1)S(1)} all-gather(bf16[256,32]{0,1:T(8,128)(2,1)S(1)} %copy-done.110), channel_id=1, replica_groups=mesh['dp'=16,'tensor'=2] {'dp'}, dimensions={1}, use_global_device_ids=true | all-gather | bytes 278528 | tf_op jit(solution)/shard_map/all_gather | solution.py:129
  361.8 39.9 %all_gather.109 = bf16[512,3,256]{2,0,1:T(8,128)(2,1)S(1)} all-gather(bf16[32,3,256]{2,0,1:T(8,128)(2,1)S(1)} %copy-done.94), channel_id=1, replica_groups=mesh['dp'=16,'tensor'=2] {'dp'}, dimensions={0}, use_global_device_ids=true | all-gather | bytes 835584 | tf_op jit(solution)/shard_map/all_gather | solution.py:127
  450.1 18.2 reshape.1822
  480.2 19.2 reshape.1823
  568.8 18.2 reshape.1825
  599.0 19.2 reshape.1826
  657.9 41.2 %all_gather.113 = bf16[13,2,128]{0,2,1:T(8,128)(2,1)S(1)} all-gather(bf16[13,2,8]{0,2,1:T(8,128)(2,1)S(1)} %copy-done.144), channel_id=1, replica_groups=mesh['dp'=16,'tensor'=2] {'dp'}, dimensions={2}, use_global_device_ids=true | all-gather | bytes 7072 | tf_op jit(solution)/shard_map/all_gather | solution.py:133
  699.3 39.2 %all_gather.116 = bf16[256,512]{0,1:T(8,128)(2,1)} all-gather(bf16[256,32]{0,1:T(8,128)(2,1)S(1)} %copy-done.111), channel_id=1, replica_groups=mesh['dp'=16,'tensor'=2] {'dp'}, dimensions={1}, use_global_device_ids=true | all-gather | bytes 278528 | tf_op jit(solution)/shard_map/all_gather | solution.py:132
  740.1 40.9 %all_gather.115 = bf16[512,2,256]{2,0,1:T(8,128)(2,1)S(1)} all-gather(bf16[32,2,256]{2,0,1:T(8,128)(2,1)S(1)} %copy.360), channel_id=1, replica_groups=mesh['dp'=16,'tensor'=2] {'dp'}, dimensions={0}, use_global_device_ids=true | all-gather | bytes 557056 | tf_op jit(solution)/shard_map/all_gather | solution.py:131
  793.5 37.7 %all-reduce.16 = (f32[256]{0:T(256)S(1)}, f32[]{:T(128)}, f32[256]{0:T(256)S(1)}, f32[256]{0:T(256)S(1)}, f32[]{:T(128)}, /*index=5*/f32[256]{0:T(256)S(1)}) all-reduce(f32[256]{0:T(256)S(1)} %get-tuple-element.299, f32[]{:T(128)} %get-tuple-element.364, f32[256]{0:T(256)S(1)} %get-tuple-element.300, ...), channel_id=1, replica_groups=mesh['dp'=16,'tensor'=2] {'dp'}, use_global_device_ids=true, to_apply=%region_33.34 | all-reduce | flops 1026 | bytes 8208 | tf_op jit(solution)/shard_map/psum | solution.py:407
  858.3 41.2 %all_gather.119 = bf16[8,128]{0,1:T(8,128)(2,1)S(1)} all-gather(bf16[8,8]{0,1:T(8,128)(2,1)S(1)} %copy.366), channel_id=1, replica_groups=mesh['dp'=16,'tensor'=2] {'dp'}, dimensions={1}, use_global_device_ids=true | all-gather | bytes 2176 | tf_op jit(solution)/shard_map/all_gather | solution.py:136
  940.8 51.4 %all-gather.35.cloned.1.call-done = bf16[1024,512]{0,1:T(8,128)(2,1)} async-done(((bf16[1024,32]{0,1:T(8,128)(2,1)}), bf16[1024,512]{0,1:T(8,128)(2,1)}) %all-gather.35.cloned.1.call-update) | async-done | bytes 1048592 | tf_op jit(solution)/shard_map/all_gather | solution.py:135
  1102.4 42.1 %all-reduce.15 = (f32[256]{0:T(256)S(1)}, f32[256]{0:T(256)S(1)}, f32[256]{0:T(256)S(1)}, f32[256]{0:T(256)S(1)}) all-reduce(f32[256]{0:T(256)S(1)} %get-tuple-element.328, f32[256]{0:T(256)S(1)} %get-tuple-element.327, f32[256]{0:T(256)S(1)} %get-tuple-element.107, ...), channel_id=1, replica_groups=mesh['dp'=16,'tensor'=2] {'dp'}, use_global_device_ids=true, to_apply=%region_71.72 | all-reduce | flops 1024 | bytes 8192 | tf_op jit(solution)/shard_map/psum | solution.py:469
  1241.7 22.1 reshape.1829
  1324.2 21.8 reshape.1832
  1525.3 72.2 %all-reduce.14 = (f32[8,128]{1,0:T(8,128)S(1)}, f32[4,2,128]{2,1,0:T(2,128)S(1)}, f32[13,2,128]{2,0,1:T(8,128)S(1)}, f32[8,128]{1,0:T(8,128)S(1)}) all-reduce(f32[8,128]{1,0:T(8,128)S(1)} %add_bitcast_fusion.1, f32[4,2,128]{2,1,0:T(2,128)S(1)} %maximum_add_fusion, ...), channel_id=20, replica_groups=mesh['dp'=16,'tensor'=2] {'dp'}, use_global_device_ids=true, to_apply=%region_86.87.clone | all-reduce | flops 6400 | bytes 51200
  1603.3 52.5 %reduce-scatter.83.cloned.1.call-done = f32[16,14]{1,0:T(8,128)} async-done(((f32[512,14]{1,0:T(8,128)}), f32[16,14]{1,0:T(8,128)}) %reduce-scatter.83.cloned.1.call-update) | async-done | bytes 912
  1657.2 78.0 %reduce-scatter.81.cloned.1.call-done = f32[1024,32]{0,1:T(8,128)} async-done(((f32[1024,512]{0,1:T(8,128)}), f32[1024,32]{0,1:T(8,128)}) %reduce-scatter.81.cloned.1.call-update) | async-done | bytes 131088 | tf_op jit(solution)/shard_map/reduce_scatter | solution.py:153
  1735.3 80.7 %reduce-scatter.79.cloned.1.call-done = f32[32,1024]{1,0:T(8,128)} async-done(((f32[512,1024]{1,0:T(8,128)}), f32[32,1024]{1,0:T(8,128)}) %reduce-scatter.79.cloned.1.call-update) | async-done | bytes 131088 | tf_op jit(solution)/shard_map/reduce_scatter | solution.py:152
  1816.0 76.4 %reduce-scatter.77.cloned.1.call-done = f32[256,32]{0,1:T(8,128)} async-done(((f32[256,512]{0,1:T(8,128)}), f32[256,32]{0,1:T(8,128)}) %reduce-scatter.77.cloned.1.call-update) | async-done | bytes 32784 | tf_op jit(solution)/shard_map/reduce_scatter | solution.py:150
  1892.3 75.8 %reduce-scatter.73.cloned.1.call-done = f32[256,32]{0,1:T(8,128)} async-done(((f32[256,512]{0,1:T(8,128)}), f32[256,32]{0,1:T(8,128)}) %reduce-scatter.73.cloned.1.call-update) | async-done | bytes 32784 | tf_op jit(solution)/shard_map/reduce_scatter | solution.py:147
  1968.2 75.6 %reduce-scatter.71.cloned.1.call-done = f32[32,256]{1,0:T(8,128)} async-done(((f32[512,256]{1,0:T(8,128)}), f32[32,256]{1,0:T(8,128)}) %reduce-scatter.71.cloned.1.call-update) | async-done | bytes 32784 | tf_op jit(solution)/shard_map/reduce_scatter | solution.py:146
  2043.8 78.3 %reduce-scatter.69.cloned.1.call-done = f32[32,3,256]{2,0,1:T(8,128)} async-done(((f32[512,3,256]{2,0,1:T(8,128)}), f32[32,3,256]{2,0,1:T(8,128)}) %reduce-scatter.69.cloned.1.call-update) | async-done | bytes 98320 | tf_op jit(solution)/shard_map/reduce_scatter | solution.py:145
  2122.1 80.0 %reduce-scatter.67.cloned.1.call-done = f32[1024,32]{0,1:T(8,128)} async-done(((f32[1024,512]{0,1:T(8,128)}), f32[1024,32]{0,1:T(8,128)}) %reduce-scatter.67.cloned.1.call-update) | async-done | bytes 131088 | tf_op jit(solution)/shard_map/reduce_scatter | solution.py:143
  2202.0 80.6 %reduce-scatter.65.cloned.1.call-done = f32[32,1024]{1,0:T(8,128)} async-done(((f32[512,1024]{1,0:T(8,128)}), f32[32,1024]{1,0:T(8,128)}) %reduce-scatter.65.cloned.1.call-update) | async-done | bytes 131088 | tf_op jit(solution)/shard_map/reduce_scatter | solution.py:142
  (784 shorter events, 764.3 us)
Async XLA Ops:
  7.2 89.6 %all-gather.21.cloned.1.call-start = ((), (), s32[]{:S(2)}) async-start(), calls=%async_computation.26 | async-start | bytes 1572864 | tf_op jit(solution)/shard_map/all_gather | solution.py:89
  58.8 64.5 %all-gather.23.cloned.1.call-start = ((), (), s32[]{:S(2)}) async-start(), calls=%async_computation.27 | async-start | bytes 1114112 | tf_op jit(solution)/shard_map/all_gather | solution.py:124
  59.5 73.8 %all-gather.37.cloned.1.call-start = ((), (), s32[]{:S(2)}) async-start(), calls=%async_computation.38 | async-start | bytes 1572864 | tf_op jit(solution)/shard_map/all_gather | solution.py:89
  60.3 132.1 %all-gather.25.cloned.1.call-start = ((), (), s32[]{:S(2)}) async-start(), calls=%async_computation.28 | async-start | bytes 1114112 | tf_op jit(solution)/shard_map/all_gather | solution.py:125
  60.9 215.6 %reduce-scatter.41.cloned.1.call-start = ((), (), s32[]{:S(2)}) async-start(), calls=%async_computation.39 | async-start | bytes 1572864 | tf_op jit(solution)/shard_map/reduce_scatter | solution.py:93
  196.7 79.8 %reduce-scatter.33.cloned.1.call-start = ((), (), s32[]{:S(2)}) async-start(), calls=%async_computation.29 | async-start | bytes 1572864 | tf_op jit(solution)/shard_map/reduce_scatter | solution.py:93
  200.6 201.1 %all-gather.39.cloned.1.call-start = ((), (), s32[]{:S(2)}) async-start(), calls=%async_computation.40 | async-start | bytes 1572864 | tf_op jit(solution)/shard_map/all_gather | solution.py:89
  281.9 123.5 %all-gather.27.cloned.1.call-start = ((), (), s32[]{:S(2)}) async-start(), calls=%async_computation.30 | async-start | bytes 1572864 | tf_op jit(solution)/shard_map/all_gather | solution.py:89
  321.9 325.4 %reduce-scatter.35.cloned.1.call-start = ((), (), s32[]{:S(2)}) async-start(), calls=%async_computation.31 | async-start | bytes 1572864 | tf_op jit(solution)/shard_map/reduce_scatter | solution.py:93
  529.9 123.6 %reduce-scatter.43.cloned.1.call-start = ((), (), s32[]{:S(2)}) async-start(), calls=%async_computation.41 | async-start | bytes 1572864 | tf_op jit(solution)/shard_map/reduce_scatter | solution.py:93
  646.8 134.2 %all-gather.41.cloned.1.call-start = ((), (), s32[]{:S(2)}) async-start(), calls=%async_computation.42 | async-start | bytes 1572864 | tf_op jit(solution)/shard_map/all_gather | solution.py:89
  657.8 127.0 %all-gather.29.cloned.1.call-start = ((), (), s32[]{:S(2)}) async-start(), calls=%async_computation.32 | async-start | bytes 1572864 | tf_op jit(solution)/shard_map/all_gather | solution.py:89
  738.5 102.7 %reduce-scatter.37.cloned.1.call-start = ((), (), s32[]{:S(2)}) async-start(), calls=%async_computation.33 | async-start | bytes 1572864 | tf_op jit(solution)/shard_map/reduce_scatter | solution.py:93
  837.8 74.4 %all-gather.33.cloned.1.call-start = ((), (), s32[]{:S(2)}) async-start(), calls=%async_computation.35 | async-start | bytes 1114112 | tf_op jit(solution)/shard_map/all_gather | solution.py:134
  838.4 83.0 %all-gather.43.cloned.1.call-start = ((), (), s32[]{:S(2)}) async-start(), calls=%async_computation.44 | async-start | bytes 1572864 | tf_op jit(solution)/shard_map/all_gather | solution.py:89
  857.0 76.1 %all-gather.31.cloned.1.call-start = ((), (), s32[]{:S(2)}) async-start(), calls=%async_computation.34 | async-start | bytes 1572864 | tf_op jit(solution)/shard_map/all_gather | solution.py:89
  857.6 134.6 %all-gather.35.cloned.1.call-start = ((), (), s32[]{:S(2)}) async-start(), calls=%async_computation.36 | async-start | bytes 1114112 | tf_op jit(solution)/shard_map/all_gather | solution.py:135
  858.2 145.7 %reduce-scatter.39.cloned.1.call-start = ((), (), s32[]{:S(2)}) async-start(), calls=%async_computation.37 | async-start | bytes 1572864 | tf_op jit(solution)/shard_map/reduce_scatter | solution.py:93
  1080.5 88.2 %reduce-scatter.51.cloned.1.call-start = ((), (), s32[]{:S(2)}) async-start(), calls=%async_computation.49 | async-start | bytes 1572864 | tf_op jit(solution)/shard_map/reduce_scatter | solution.py:103
  1184.9 195.0 %reduce-scatter.53.cloned.1.call-start = ((), (), s32[]{:S(2)}) async-start(), calls=%async_computation.51 | async-start | bytes 1572864 | tf_op jit(solution)/shard_map/reduce_scatter | solution.py:103
  1296.4 93.3 %reduce-scatter.61.cloned.1.call-start = ((), (), s32[]{:S(2)}) async-start(), calls=%async_computation.59 | async-start | bytes 1572864 | tf_op jit(solution)/shard_map/reduce_scatter | solution.py:103
  1396.8 39.0 %reduce-scatter.55.cloned.1.call-start = ((), (), s32[]{:S(2)}) async-start(), calls=%async_computation.53 | async-start | bytes 1572864 | tf_op jit(solution)/shard_map/reduce_scatter | solution.py:103
  1426.9 96.2 %reduce-scatter.75.cloned.1.call-start = ((), (), s32[]{:S(2)}) async-start(), calls=%async_computation.67 | async-start | bytes 1114112 | tf_op jit(solution)/shard_map/reduce_scatter | solution.py:149
  1431.3 224.6 %reduce-scatter.83.cloned.1.call-start = ((), (), s32[]{:S(2)}) async-start(), calls=%async_computation.71 | async-start | bytes 270336
  1445.6 289.6 %reduce-scatter.81.cloned.1.call-start = ((), (), s32[]{:S(2)}) async-start(), calls=%async_computation.70 | async-start | bytes 2228224 | tf_op jit(solution)/shard_map/reduce_scatter | solution.py:153
  1450.9 365.1 %reduce-scatter.79.cloned.1.call-start = ((), (), s32[]{:S(2)}) async-start(), calls=%async_computation.69 | async-start | bytes 2228224 | tf_op jit(solution)/shard_map/reduce_scatter | solution.py:152
  1456.7 435.6 %reduce-scatter.77.cloned.1.call-start = ((), (), s32[]{:S(2)}) async-start(), calls=%async_computation.68 | async-start | bytes 557056 | tf_op jit(solution)/shard_map/reduce_scatter | solution.py:150
  1461.8 506.4 %reduce-scatter.73.cloned.1.call-start = ((), (), s32[]{:S(2)}) async-start(), calls=%async_computation.66 | async-start | bytes 557056 | tf_op jit(solution)/shard_map/reduce_scatter | solution.py:147
  1474.1 569.7 %reduce-scatter.71.cloned.1.call-start = ((), (), s32[]{:S(2)}) async-start(), calls=%async_computation.65 | async-start | bytes 557056 | tf_op jit(solution)/shard_map/reduce_scatter | solution.py:146
  1483.5 638.6 %reduce-scatter.69.cloned.1.call-start = ((), (), s32[]{:S(2)}) async-start(), calls=%async_computation.64 | async-start | bytes 1671168 | tf_op jit(solution)/shard_map/reduce_scatter | solution.py:145
  1488.6 713.4 %reduce-scatter.67.cloned.1.call-start = ((), (), s32[]{:S(2)}) async-start(), calls=%async_computation.63 | async-start | bytes 2228224 | tf_op jit(solution)/shard_map/reduce_scatter | solution.py:143
  1496.2 786.5 %reduce-scatter.65.cloned.1.call-start = ((), (), s32[]{:S(2)}) async-start(), calls=%async_computation.62 | async-start | bytes 2228224 | tf_op jit(solution)/shard_map/reduce_scatter | solution.py:142
  (219 other events, 4708.7 us)
Sparse Core Ops, SparseCore 0:
  66.9 56.4 all-gather.22
  135.9 56.4 all-gather.24
  657.9 10.1 all-gather.40
  843.3 9.6 reduce-scatter.44
  855.7 56.4 all-gather.32
  922.9 10.1 all-gather.30
  935.7 56.4 all-gather.34
  1022.8 10.1 all-gather.44
  1034.6 10.1 all-gather.52
  1047.1 9.6 reduce-scatter.48
  1059.0 9.6 reduce-scatter.56
  1076.0 10.1 all-gather.54
  1087.7 10.1 all-gather.46
  1169.0 9.6 reduce-scatter.58
  1181.9 10.1 all-gather.48
  1193.5 10.1 all-gather.56
  1296.5 9.6 reduce-scatter.52
  1379.9 9.6 reduce-scatter.60
  1396.2 10.1 all-gather.50
  1408.0 10.1 all-gather.58
  1420.4 9.6 reduce-scatter.54
  1432.4 9.6 reduce-scatter.62
  1444.2 78.8 reduce-scatter.74
  1525.4 130.3 reduce-scatter.82
  1658.6 76.6 reduce-scatter.80
  1738.1 77.7 reduce-scatter.78
  1818.8 73.5 reduce-scatter.76
  1895.2 72.8 reduce-scatter.72
  1970.8 72.8 reduce-scatter.70
  2046.7 75.3 reduce-scatter.68
  2124.8 77.2 reduce-scatter.66
  2204.7 77.9 reduce-scatter.64
  (14 shorter events, 96.7 us)
where the time goes:
time: 2300 us; the launch traced here: 2290 us
  waiting for transfers between devices  983 us (43%)
  blocking collectives  549 us (24%)
  local copies, waits for them, and re-layouts  348 us (15%)
  matrix products  251 us (11%)
  other arithmetic  136 us (6%)
    unnamed x431, local copies, waits for them, and re-layouts  94.7 us
    reshape x4, local copies, waits for them, and re-layouts, rel_shift(): padded[..., 1:, :].reshape(leading + (row_count, col_count))  82.3 us
    reduce_scatter x1, waiting for transfers between devices, reduce_grads(): lax.psum_scatter(packed[10], 'dp', scatter_dimension=0, tiled=True)  80.7 us
    reduce_scatter x1, waiting for transfers between devices, reduce_grads(): lax.psum_scatter(packed[0], 'dp', scatter_dimension=0, tiled=True)  80.6 us
    reduce_scatter x1, waiting for transfers between devices, reduce_grads(): lax.psum_scatter(packed[1], 'dp', scatter_dimension=1, tiled=True)  80 us
    reduce_scatter x1, waiting for transfers between devices, reduce_grads(): lax.psum_scatter(packed[3], 'dp', scatter_dimension=0, tiled=True)  78.3 us
    reduce_scatter x1, waiting for transfers between devices, reduce_grads(): lax.psum_scatter(packed[11], 'dp', scatter_dimension=1, tiled=True)  78 us
    reduce_scatter x1, waiting for transfers between devices, reduce_grads(): lax.psum_scatter(packed[8], 'dp', scatter_dimension=1, tiled=True)  76.4 us
  transfers between devices with their start and end apart: 46, of which 34 were waited for; matrix products, arithmetic and copies ran while one was open for 19% of the time, Pallas kernels for 0%

commit v1 on v0

v1 whole, which is shorter than its diff:
```python
import math

import jax
import jax.numpy as jnp
from jax import lax
from jax.experimental import pallas as pl
from jax.experimental.pallas import tpu as pltpu
from jax.sharding import PartitionSpec as P

DK = 64
norm_eps = 1e-05
mask_fill = -1000000000.0
BF = jnp.bfloat16
F32 = jnp.float32
BLK = 128


def nn(a, b):
    return lax.dot_general(a, b, (((1,), (0,)), ((), ())), preferred_element_type=F32)


def nt(a, b):
    return lax.dot_general(a, b, (((1,), (1,)), ((), ())), preferred_element_type=F32)


def tn(a, b):
    return lax.dot_general(a, b, (((0,), (0,)), ((), ())), preferred_element_type=F32)


def position_table(length, width):
    cols = jnp.arange(width, dtype=jnp.int32)
    rate = jnp.exp((cols // 2 * 2).astype(F32) * (-math.log(10000.0) / width))[None, :]
    phase = (cols % 2).astype(F32)[None, :] * (0.5 * math.pi)
    step = 32
    coarse = (length - 1 - step * jnp.arange(2 * length // step, dtype=jnp.int32)).astype(F32)
    fine = jnp.arange(step, dtype=jnp.int32).astype(F32)
    big = coarse[:, None] * rate
    small = fine[:, None] * rate
    even = (cols % 2 == 0)[None, :]
    sin_big, cos_big = jnp.sin(big), jnp.cos(big)
    first = jnp.where(even, sin_big, cos_big)
    second = jnp.where(even, cos_big, -sin_big)
    rows = first[:, None] * jnp.cos(small)[None] - second[:, None] * jnp.sin(small)[None]
    return rows.reshape(2 * length, width)


def swish_act(values):
    return values * jax.nn.sigmoid(values)


def swish_slope(values):
    sigma = jax.nn.sigmoid(values)
    return sigma + values * sigma * (1.0 - sigma)


def norm_forward(values, gain, shift):
    average = jnp.mean(values, axis=-1, keepdims=True)
    centered = values - average
    inv_std = lax.rsqrt(jnp.mean(centered * centered, axis=-1, keepdims=True) + norm_eps)
    scaled = centered * inv_std
    return (scaled * gain + shift, scaled, inv_std)


def norm_backward(upstream, scaled, inv_std, gain):
    grad_gain = jnp.sum(upstream * scaled, axis=(0, 1))
    grad_shift = jnp.sum(upstream, axis=(0, 1))
    grad_scaled = upstream * gain
    inner = (
        grad_scaled
        - jnp.mean(grad_scaled, axis=-1, keepdims=True)
        - scaled * jnp.mean(grad_scaled * scaled, axis=-1, keepdims=True)
    )
    return (inv_std * inner, grad_gain, grad_shift)


def depthwise(signal, taps_all):
    reach = (taps_all.shape[0] - 1) // 2
    length_now = signal.shape[1]
    padded = jnp.pad(signal, ((0, 0), (reach, reach), (0, 0)))
    summed = jnp.zeros_like(signal)
    for tap_idx in range(taps_all.shape[0]):
        summed = summed + taps_all[tap_idx] * padded[:, tap_idx : tap_idx + length_now]
    return summed


def depthwise_back(upstream, signal, taps_all):
    reach = (taps_all.shape[0] - 1) // 2
    length_now = upstream.shape[1]
    padded_grad = jnp.pad(upstream, ((0, 0), (reach, reach), (0, 0)))
    padded_sig = jnp.pad(signal, ((0, 0), (reach, reach), (0, 0)))
    grad_signal = jnp.zeros_like(signal)
    tap_grads = []
    for tap_idx in range(taps_all.shape[0]):
        begin = 2 * reach - tap_idx
        grad_signal = grad_signal + taps_all[tap_idx] * padded_grad[:, begin : begin + length_now]
        tap_grads.append(
            jnp.sum(upstream * padded_sig[:, tap_idx : tap_idx + length_now], axis=(0, 1))
        )
    return (grad_signal, jnp.stack(tap_grads))


def attn_fwd_kernel(len_ref, qu, qv, k, v, pos, o_ref, lse_ref):
    count = len_ref[pl.program_id(0)]
    full = k.shape[1]
    lane = lax.broadcasted_iota(jnp.int32, (BLK, 2 * DK), 1)
    col = lax.broadcasted_iota(jnp.int32, (BLK, full), 1)
    keep = col < count
    zero = jnp.zeros((), BF)
    for blk in range(full // BLK):
        i0 = blk * BLK
        base = full - BLK - i0
        outs, logs = [], []
        for h in range(2):
            mine = (lane < DK) if h == 0 else (lane >= DK)
            q_u = jnp.where(mine, qu[0, i0 : i0 + BLK, :], zero)
            q_v = jnp.where(mine, qv[0, i0 : i0 + BLK, :], zero)
            rel = nt(q_v, pos[base : base + full + BLK, :])
            rel = pltpu.roll(rel, full + 1, 1, stride=1, stride_axis=0)[:, :full]
            s = (nt(q_u, k[0]) + rel) * (1.0 / math.sqrt(DK))
            s = jnp.where(keep, s, mask_fill)
            top = jnp.max(s, axis=1, keepdims=True)
            e = jnp.exp(s - top)
            total = jnp.sum(e, axis=1, keepdims=True)
            outs.append(nn(e.astype(BF), v[0]) / total)
            logs.append(top + jnp.log(total))
        left = lane < DK
        o_ref[0, i0 : i0 + BLK, :] = jnp.where(left, outs[0], outs[1]).astype(BF)
        lse_ref[0, i0 : i0 + BLK, :] = jnp.where(left, logs[0], logs[1])


def attn_bwd_kernel(
    len_ref, qu, qv, k, v, pos, o, lse, do, dq_ref, dk_ref, dv_ref, dpos_ref, sum_ref, dkt, dvt, dpt
):
    count = len_ref[pl.program_id(0)]
    full = k.shape[1]
    scale = 1.0 / math.sqrt(DK)
    lane = lax.broadcasted_iota(jnp.int32, (BLK, 2 * DK), 1)
    left = lane < DK
    keep = lax.broadcasted_iota(jnp.int32, (BLK, full), 1) < count
    zero = jnp.zeros((), BF)
    flip = (lane + lax.broadcasted_iota(jnp.int32, (BLK, 2 * DK), 0) == BLK - 1).astype(F32).astype(BF)
    dkt[...] = jnp.zeros_like(dkt)
    dvt[...] = jnp.zeros_like(dvt)
    dpt[...] = jnp.zeros_like(dpt)
    sum_q = jnp.zeros((1, 2 * DK), F32)
    sum_u = jnp.zeros((1, 2 * DK), F32)
    sum_v = jnp.zeros((1, 2 * DK), F32)
    for blk in range(full // BLK):
        i0 = blk * BLK
        base = full - BLK - i0
        rows = slice(i0, i0 + BLK)
        win = slice(base, base + full + BLK)
        qu_t = qu[0, rows, :].astype(F32).T.astype(BF)
        do_t = do[0, rows, :].astype(F32).T.astype(BF)
        qv_t = tn(qv[0, rows, :], flip).astype(BF)
        dot_o = do[0, rows, :].astype(F32) * o[0, rows, :].astype(F32)
        parts_u, parts_v = [], []
        for h in range(2):
            mine = left if h == 0 else lane >= DK
            hs = slice(h * DK, h * DK + DK)
            q_u = jnp.where(mine, qu[0, rows, :], zero)
            q_v = jnp.where(mine, qv[0, rows, :], zero)
            d_o = jnp.where(mine, do[0, rows, :], zero)
            rel = nt(q_v, pos[win, :])
            rel = pltpu.roll(rel, full + 1, 1, stride=1, stride_axis=0)[:, :full]
            s = (nt(q_u, k[0]) + rel) * scale - lse[0, rows, h * DK : h * DK + 1]
            p = jnp.where(keep, jnp.exp(jnp.minimum(s, 0.0)), 0.0)
            delta = jnp.sum(jnp.where(mine, dot_o, 0.0), axis=1, keepdims=True)
            ds = (p * (nt(d_o, v[0]) - delta)).astype(BF)
            dvt[hs, :] += nn(do_t[hs, :], p.astype(BF))
            dkt[hs, :] += nn(qu_t[hs, :], ds)
            parts_u.append(nn(ds, k[0]))
            wide = jnp.concatenate([nn(flip, ds), jnp.zeros((BLK, BLK), F32)], axis=1)
            wide = pltpu.roll(wide, 0, 1, stride=1, stride_axis=0).astype(BF)
            parts_v.append(nn(wide, pos[win, :]))
            dpt[hs, win] += nn(qv_t[hs, :], wide)
        d_u = jnp.where(left, parts_u[0], parts_u[1]) * scale
        d_v = jnp.where(left, parts_v[0], parts_v[1]) * scale
        high = d_v.astype(BF)
        low = (d_v - high.astype(F32)).astype(BF)
        d_q = (d_u + nn(flip, high) + nn(flip, low)).astype(BF)
        dq_ref[0, rows, :] = d_q
        sum_q += jnp.sum(d_q.astype(F32), axis=0, keepdims=True)
        sum_u += jnp.sum(d_u, axis=0, keepdims=True)
        sum_v += jnp.sum(d_v, axis=0, keepdims=True)
    dk_ref[0] = (dkt[...].T * scale).astype(BF)
    d_val = dvt[...].T.astype(BF)
    dv_ref[0] = d_val
    dpos_ref[0] = (dpt[...].T * scale).astype(BF)
    sum_ref[0, 0:1, :] = sum_q
    sum_ref[0, 1:2, :] = jnp.sum(d_val.astype(F32), axis=0, keepdims=True)
    sum_ref[0, 2:3, :] = sum_u
    sum_ref[0, 3:4, :] = sum_v
    sum_ref[0, 4:8, :] = jnp.zeros((4, 2 * DK), F32)


def attn_specs(rows, full, width):
    pairs = width // (2 * DK)
    main = pl.BlockSpec((1, full, 2 * DK), lambda u, p, n: (u, 0, p))
    pos = pl.BlockSpec((2 * full, 2 * DK), lambda u, p, n: (0, p))
    return (rows, pairs), main, pos


def attn_fwd_call(lens, qu, qv, k, v, pos):
    rows, full, width = qu.shape
    grid, main, pspec = attn_specs(rows, full, width)
    return pl.pallas_call(
        attn_fwd_kernel,
        grid_spec=pltpu.PrefetchScalarGridSpec(
            num_scalar_prefetch=1,
            grid=grid,
            in_specs=[main] * 4 + [pspec],
            out_specs=[main, main],
        ),
        out_shape=[
            jax.ShapeDtypeStruct((rows, full, width), BF),
            jax.ShapeDtypeStruct((rows, full, width), F32),
        ],
        name="attn_fwd",
    )(lens, qu, qv, k, v, pos)


def attn_bwd_call(lens, qu, qv, k, v, pos, o, lse, do):
    rows, full, width = qu.shape
    grid, main, pspec = attn_specs(rows, full, width)
    return pl.pallas_call(
        attn_bwd_kernel,
        grid_spec=pltpu.PrefetchScalarGridSpec(
            num_scalar_prefetch=1,
            grid=grid,
            in_specs=[main] * 4 + [pspec] + [main] * 3,
            out_specs=[
                main,
                main,
                main,
                pl.BlockSpec((1, 2 * full, 2 * DK), lambda u, p, n: (u, 0, p)),
                pl.BlockSpec((1, 8, 2 * DK), lambda u, p, n: (u, 0, p)),
            ],
            scratch_shapes=[
                pltpu.VMEM((2 * DK, full), F32),
                pltpu.VMEM((2 * DK, full), F32),
                pltpu.VMEM((2 * DK, 2 * full), F32),
            ],
        ),
        out_shape=[jax.ShapeDtypeStruct((rows, full, width), BF)] * 3
        + [
            jax.ShapeDtypeStruct((rows, 2 * full, width), BF),
            jax.ShapeDtypeStruct((rows, 8, width), F32),
        ],
        name="attn_bwd",
    )(lens, qu, qv, k, v, pos, o, lse, do)


def ffn_forward(residual, gain, shift, out_bias, weights):
    w_in, w_out_t, b_in = weights
    normed, scaled, inv_std = norm_forward(residual, gain, shift)
    hn = normed.astype(BF)
    zf = jnp.einsum("uth,hf->utf", hn, w_in, preferred_element_type=F32) + b_in
    af = swish_act(zf).astype(BF)
    out = jnp.einsum("utf,hf->uth", af, w_out_t, preferred_element_type=F32) + out_bias
    return out, (scaled, inv_std, hn, zf, af)


def ffn_backward(upstream, kept, gain, weights):
    scaled, inv_std, hn, zf, af = kept
    w_in, w_out_t, b_in = weights
    g = upstream.astype(BF)
    g_bias = jnp.sum(g.astype(F32), axis=(0, 1))
    g_out = jnp.einsum("uth,utf->hf", g, af, preferred_element_type=F32)
    d_af = jnp.einsum("uth,hf->utf", g, w_out_t, preferred_element_type=F32)
    dz = (d_af * swish_slope(zf)).astype(BF)
    g_b = jnp.sum(dz.astype(F32), axis=(0, 1))
    g_in = jnp.einsum("uth,utf->hf", hn, dz, preferred_element_type=F32)
    d_hn = jnp.einsum("utf,hf->uth", dz, w_in, preferred_element_type=F32)
    d_x, g_gain, g_shift = norm_backward(d_hn, scaled, inv_std, gain)
    return d_x, (g_in, g_out, g_b), (g_gain, g_shift, g_bias)


SEGS = ("f1i", "f1o", "qkv", "pos", "out", "ci", "co", "f2i", "f2o")


def local(
    frames,
    lengths,
    ffn1_in,
    ffn1_out,
    ffn1_bias,
    qkv_weight,
    pos_weight,
    out_weight,
    attn_bias,
    conv_in,
    conv_out,
    conv_channel,
    ffn2_in,
    ffn2_out,
    ffn2_bias,
    norm_params,
    cotangent,
):
    micro, seqs, full, width = frames.shape
    both = ("dp", "tensor")
    n_dp = lax.axis_size("dp")
    rows = ffn1_in.shape[0]
    batch = micro * seqs
    shards = (
        ffn1_in,
        ffn1_out.T,
        qkv_weight.reshape(rows, -1),
        pos_weight,
        out_weight.T,
        conv_in.reshape(rows, -1),
        conv_out.T,
        ffn2_in,
        ffn2_out.T,
    )
    sizes = [item.shape[1] for item in shards]
    starts = [sum(sizes[:i]) for i in range(len(sizes))]
    packed = jnp.concatenate(shards, axis=1)
    every = lax.all_gather(packed, both, axis=0, tiled=True)
    every = every.reshape(n_dp, 2, rows, -1).transpose(1, 0, 2, 3).reshape(2, n_dp * rows, -1)
    full_w = {}
    for name, start, size in zip(SEGS, starts, sizes):
        full_w[name] = (every[0, :, start : start + size], every[1, :, start : start + size])
    small = jnp.concatenate(
        [item.reshape(-1) for item in (ffn1_bias, attn_bias, conv_channel, ffn2_bias, norm_params)]
    )
    smalls = lax.all_gather(small, both, axis=0, tiled=False).reshape(n_dp, 2, -1).astype(F32)

    def take(item, offset):
        return smalls[:, :, offset : offset + item.size].reshape((n_dp, 2) + item.shape)

    off = 0
    pieces = []
    for item in (ffn1_bias, attn_bias, conv_channel, ffn2_bias, norm_params):
        pieces.append(take(item, off))
        off += item.size
    b1 = pieces[0].transpose(1, 2, 0, 3).reshape(-1)
    vec = pieces[1].transpose(2, 1, 3, 0, 4).reshape(attn_bias.shape[0], -1)
    cvec = pieces[2].transpose(2, 1, 3, 0, 4).reshape(conv_channel.shape[0], -1)
    b2 = pieces[3].transpose(1, 2, 0, 3).reshape(-1)
    norms = pieces[4].transpose(2, 0, 1, 3).reshape(norm_params.shape[0], -1)

    def cat(name):
        return jnp.concatenate(full_w[name], axis=1)

    def cat3(name, parts):
        pair = [item.reshape(item.shape[0], parts, -1) for item in full_w[name]]
        return jnp.concatenate(pair, axis=2)

    ffn1_w = (cat("f1i"), cat("f1o"), b1)
    ffn2_w = (cat("f2i"), cat("f2o"), b2)
    w_qkv, w_pos, w_out_t = cat3("qkv", 3), cat("pos"), cat("out")
    w_ci, w_co_t = cat3("ci", 2), cat("co")
    mine = lax.axis_index("tensor")
    lens = lax.dynamic_slice_in_dim(lengths, mine * seqs, seqs, 1).reshape(-1)
    positions = jnp.arange(full, dtype=jnp.int32)
    valid = (positions[None, :] < lens[:, None]).astype(F32)
    mask3 = valid[:, :, None]
    table = position_table(full, width).astype(BF)
    x0 = frames.reshape(batch, full, width).astype(F32)
    y1, kept1 = ffn_forward(x0, norms[0], norms[1], norms[2], ffn1_w)
    x1 = x0 + 0.5 * y1
    normed, scaled2, inv2 = norm_forward(x1, norms[3], norms[4])
    hn2 = normed.astype(BF)
    proj = jnp.einsum("uth,hkc->utkc", hn2, w_qkv, preferred_element_type=F32)
    query = proj[:, :, 0] + vec[0]
    keys = proj[:, :, 1].astype(BF)
    values = (proj[:, :, 2] + vec[1]).astype(BF)
    q_u = (query + vec[2]).astype(BF)
    q_v = (query + vec[3]).astype(BF)
    pos = jnp.dot(table, w_pos, preferred_element_type=F32).astype(BF)
    mixed, lse = attn_fwd_call(lens, q_u, q_v, keys, values, pos)
    y2 = jnp.einsum("utc,hc->uth", mixed, w_out_t, preferred_element_type=F32) + norms[5]
    x2 = x1 + y2
    normed, scaled3, inv3 = norm_forward(x2, norms[6], norms[7])
    hn3 = normed.astype(BF)
    halves = jnp.einsum("uth,hkc->utkc", hn3, w_ci, preferred_element_type=F32) + cvec[0:2]
    gate = jax.nn.sigmoid(halves[:, :, 1])
    gated = halves[:, :, 0] * gate * mask3
    conv = depthwise(gated, cvec[4:])

    def by_micro(item):
        return jnp.sum(item.reshape(micro, seqs, full, width), axis=(1, 2))

    stats = lax.psum(
        jnp.stack(
            [
                by_micro(conv * mask3),
                by_micro(conv * conv * mask3),
                by_micro(jnp.broadcast_to(mask3, conv.shape)),
            ]
        ),
        both,
    )
    avg = stats[0] / stats[2]
    var = stats[1] / stats[2] - avg * avg
    rstd = lax.rsqrt(var + norm_eps)

    def spread(item):
        return jnp.repeat(item, seqs, axis=0)[:, None, :]

    yhat = (conv - spread(avg)) * spread(rstd)
    bn = yhat * cvec[2] + cvec[3]
    act = swish_act(bn).astype(BF)
    y3 = jnp.einsum("utc,hc->uth", act, w_co_t, preferred_element_type=F32) + norms[8]
    x3 = x2 + y3
    y4, kept4 = ffn_forward(x3, norms[9], norms[10], norms[11], ffn2_w)
    x4 = x3 + 0.5 * y4
    result, scaled5, inv5 = norm_forward(x4, norms[12], norms[13])
    seed = cotangent.reshape(batch, full, width).astype(F32) * mask3
    d4, g12, g13 = norm_backward(seed, scaled5, inv5, norms[12])
    delta, grads_f2, norms_f2 = ffn_backward(0.5 * d4, kept4, norms[9], ffn2_w)
    d3 = d4 + delta
    g = d3.astype(BF)
    g8 = jnp.sum(g.astype(F32), axis=(0, 1))
    g_co = jnp.einsum("uth,utc->hc", g, act, preferred_element_type=F32)
    d_bn = jnp.einsum("uth,hc->utc", g, w_co_t, preferred_element_type=F32) * swish_slope(bn)
    g_scale = jnp.sum(d_bn * yhat, axis=(0, 1))
    g_offset = jnp.sum(d_bn, axis=(0, 1))
    d_yhat = d_bn * cvec[2]
    sums = lax.psum(jnp.stack([by_micro(d_yhat), by_micro(d_yhat * yhat)]), both)
    d_conv = spread(rstd) * (
        d_yhat - mask3 * (spread(sums[0]) + yhat * spread(sums[1])) / spread(stats[2])
    )
    d_gated, g_taps = depthwise_back(d_conv, gated, cvec[4:])
    d_glu = d_gated * mask3
    d_half = jnp.stack(
        [d_glu * gate, d_glu * halves[:, :, 0] * gate * (1.0 - gate)], axis=2
    ).astype(BF)
    g_cbias = jnp.sum(d_half.astype(F32), axis=(0, 1))
    g_ci = jnp.einsum("uth,utkc->hkc", hn3, d_half, preferred_element_type=F32)
    d_hn3 = jnp.einsum("utkc,hkc->uth", d_half, w_ci, preferred_element_type=F32)
    delta, g6, g7 = norm_backward(d_hn3, scaled3, inv3, norms[6])
    d2 = d3 + delta
    g = d2.astype(BF)
    g5 = jnp.sum(g.astype(F32), axis=(0, 1))
    g_out = jnp.einsum("uth,utc->hc", g, mixed, preferred_element_type=F32)
    d_mixed = jnp.einsum("uth,hc->utc", g, w_out_t, preferred_element_type=F32).astype(BF)
    dq, dk, dv, dpos, asums = attn_bwd_call(
        lens, q_u, q_v, keys, values, pos, mixed, lse, d_mixed
    )
    g_vec = jnp.sum(asums, axis=0)[0:4]
    g_pos = jnp.einsum("ph,upc->hc", table, dpos, preferred_element_type=F32)
    d_proj = jnp.stack([dq, dk, dv], axis=2)
    g_qkv = jnp.einsum("uth,utkc->hkc", hn2, d_proj, preferred_element_type=F32)
    d_hn2 = jnp.einsum("utkc,hkc->uth", d_proj, w_qkv, preferred_element_type=F32)
    delta, g3, g4 = norm_backward(d_hn2, scaled2, inv2, norms[3])
    d1 = d2 + delta
    delta, grads_f1, norms_f1 = ffn_backward(0.5 * d1, kept1, norms[0], ffn1_w)
    d0 = (d1 + delta).astype(BF)
    g_norm = jnp.stack(
        norms_f1 + (g3, g4, g5) + (g6, g7, g8) + norms_f2 + (g12, g13)
    )
    g_cvec = jnp.concatenate([g_cbias, g_scale[None], g_offset[None], g_taps], axis=0)

    def half(item, t):
        part = item.reshape(item.shape[0], -1, item.shape[-1])
        step = part.shape[-1] // 2
        return part[:, :, t * step : (t + 1) * step].reshape(n_dp, rows, -1)

    wide = (
        grads_f1[0], grads_f1[1], g_qkv, g_pos, g_out, g_ci, g_co, grads_f2[0], grads_f2[1],
    )
    grads = jnp.stack(
        [jnp.concatenate([half(item, t) for item in wide], axis=2).astype(BF) for t in (0, 1)],
        axis=1,
    ).reshape(n_dp * 2 * rows, -1)
    own = lax.psum_scatter(grads, both, scatter_dimension=0, tiled=True).astype(F32)
    outs = [own[:, start : start + size] for start, size in zip(starts, sizes)]
    tiny = lax.psum(
        jnp.concatenate(
            [item.reshape(-1) for item in (grads_f1[2], grads_f2[2], g_vec, g_cvec, g_norm)]
        ),
        both,
    )
    at = lax.axis_index("dp")

    def owned(offset, like, lead):
        groups = 2 * like.shape[-2]
        area = tiny[offset : offset + lead * groups * 128].reshape(lead, groups, 128)
        area = lax.dynamic_slice_in_dim(area, mine * like.shape[-2], like.shape[-2], 1)
        return lax.dynamic_slice_in_dim(area, at * like.shape[-1], like.shape[-1], 2).reshape(
            like.shape
        )

    o1 = 0
    o2 = grads_f1[2].size
    o3 = o2 + grads_f2[2].size
    o4 = o3 + g_vec.size
    o5 = o4 + g_cvec.size
    gn = tiny[o5 : o5 + g_norm.size].reshape(g_norm.shape)
    cols = norm_params.shape[1]
    gn = lax.dynamic_slice_in_dim(gn, (at * 2 + mine) * cols, cols, 1)
    return (
        result.astype(BF).reshape(frames.shape),
        d0.reshape(frames.shape),
        outs[0],
        outs[1].T,
        owned(o1, ffn1_bias, 1),
        outs[2].reshape(qkv_weight.shape),
        outs[3],
        outs[4].T,
        owned(o3, attn_bias, attn_bias.shape[0]),
        outs[5].reshape(conv_in.shape),
        outs[6].T,
        owned(o4, conv_channel, conv_channel.shape[0]),
        outs[7],
        outs[8].T,
        owned(o2, ffn2_bias, 1),
        gn,
    )


def solution(mesh):
    in_specs = (
        P(None, ("dp", "tensor"), None, None),
        P(None, "dp"),
        P("dp", "tensor"),
        P("tensor", "dp"),
        P("tensor", "dp"),
        P("dp", None, "tensor"),
        P("dp", "tensor"),
        P("tensor", "dp"),
        P(None, "tensor", "dp"),
        P("dp", None, "tensor"),
        P("tensor", "dp"),
        P(None, "tensor", "dp"),
        P("dp", "tensor"),
        P("tensor", "dp"),
        P("tensor", "dp"),
        P(None, ("dp", "tensor")),
        P(None, ("dp", "tensor"), None, None),
    )
    out_specs = (
        P(None, ("dp", "tensor"), None, None),
        P(None, ("dp", "tensor"), None, None),
        P("dp", "tensor"),
        P("tensor", "dp"),
        P("tensor", "dp"),
        P("dp", None, "tensor"),
        P("dp", "tensor"),
        P("tensor", "dp"),
        P(None, "tensor", "dp"),
        P("dp", None, "tensor"),
        P("tensor", "dp"),
        P(None, "tensor", "dp"),
        P("dp", "tensor"),
        P("tensor", "dp"),
        P("tensor", "dp"),
        P(None, ("dp", "tensor")),
    )
    return jax.shard_map(local, mesh=mesh, in_specs=in_specs, out_specs=out_specs, check_vma=False)
```

time: 2300 us -> 793 us (0.34)
  waiting for transfers between devices: 983 us -> 293 us
  blocking collectives: 549 us -> 123 us
  local copies, waits for them, and re-layouts: 348 us -> 120 us
  matrix products: 251 us -> 89.3 us
  Pallas kernels: 0 us -> 82.9 us
  other arithmetic: 136 us -> 61.1 us
    reduce_scatter x25 -> x1, waiting for transfers between devices: 715 us -> 158 us  [local(): lax.psum_scatter(grads, both, scatter_dimension=0, tiled=True).astype(F32)]
    all_gather x10 -> x0, blocking collectives: 397 us -> none  [the longest x1 43.6 us: local(): lax.all_gather(norm_params, ('dp', 'tensor'), axis=1, tiled=True)]
    all_gather x20 -> x1, waiting for transfers between devices: 210 us -> 38.6 us  [local(): every = lax.all_gather(packed, both, axis=0, tiled=True)]
    dot_general x69 -> x26, matrix products: 251 us -> 89.3 us  [the longest x2 12.6 us: ffn_forward(): zf = jnp.einsum('uth,hf->utf', hn, w_in, preferred_element_type=F32) + b_in]
    reshape x8 -> x15, local copies, waits for them, and re-layouts: 145 us -> 14 us  [the longest x1 6.54 us: local(): every.reshape(n_dp, 2, rows, -1).transpose(1, 0, 2, 3)]
    psum x0 -> x1, waiting for transfers between devices: none -> 96.7 us  [local(): lax.psum(jnp.concatenate([item.reshape(-1) for item in (grads_f1[2], grad...]
    pallas_call x0 -> x2, Pallas kernels: none -> 82.9 us  [the longest x1 53.6 us: attn_bwd_call(): pl.pallas_call(attn_bwd_kernel, grid_spec=pltpu.PrefetchScalarGridSpec(nu...]
    unnamed x47 -> x3, waiting for transfers between devices: 58 us -> 0.05 us
  transfers between devices with their start and end apart: 46 -> 3, of which waited for: 34 -> 3; matrix products, arithmetic and copies ran while one was open for 19% -> 5% of each run, Pallas kernels for 0% -> 0%
where the time goes in v1:
time: 793 us; the launch traced here: 786 us
  waiting for transfers between devices  293 us (37%)
  blocking collectives  123 us (16%)
  local copies, waits for them, and re-layouts  120 us (15%)
  matrix products  89.3 us (11%)
  Pallas kernels  82.9 us (10%)
  other arithmetic  61.1 us (8%)
  between operations  15.6 us (2%)
    reduce_scatter x1, waiting for transfers between devices, local(): lax.psum_scatter(grads, both, scatter_dimension=0, tiled=True).astype(F32)  158 us
    psum x1, waiting for transfers between devices, local(): lax.psum(jnp.concatenate([item.reshape(-1) for item in (grads_f1[2], grad...  96.7 us
    pallas_call x1, Pallas kernels, attn_bwd_call(): pl.pallas_call(attn_bwd_kernel, grid_spec=pltpu.PrefetchScalarGridSpec(nu...  53.6 us
    unnamed x1, blocking collectives  43.2 us
    psum x1, blocking collectives, local(): lax.psum(jnp.stack([by_micro(d_yhat), by_micro(d_yhat * yhat)]), both)  40.8 us
    unnamed x253, local copies, waits for them, and re-layouts  39.6 us
    psum x1, blocking collectives, local(): lax.psum(jnp.stack([by_micro(conv * mask3), by_micro(conv * conv * mask3)...  38.9 us
    all_gather x1, waiting for transfers between devices, local(): every = lax.all_gather(packed, both, axis=0, tiled=True)  38.6 us
  transfers between devices with their start and end apart: 3, of which 3 were waited for; matrix products, arithmetic and copies ran while one was open for 5% of the time, Pallas kernels for 0%

profile of v1, /device:TPU:0, one launch (start us, length us, event | category | flops | bytes accessed | tf_op | source)
XLA Modules:
  0.0 785.5 jit_solution(6736021188500572908)
XLA Ops:
  19.5 43.2 %all-reduce.2 = bf16[19968]{0:T(1024)(128)(2,1)S(1)} all-reduce(bf16[19968]{0:T(1024)(128)(2,1)S(1)} %dynamic-update-slice), channel_id=2, replica_groups=mesh['dp'=16,'tensor'=2] {'dp','tensor'}, use_global_device_ids=true, to_apply=%add.2 | all-reduce | flops 19968 | bytes 79872
  76.3 38.6 %all-gather.3.cloned.1.call-done = bf16[1024,6144]{1,0:T(8,128)(2,1)} async-done(((bf16[32,6144]{1,0:T(8,128)(2,1)}), bf16[1024,6144]{1,0:T(8,128)(2,1)}) %all-gather.3.cloned.1.call-update) | async-done | bytes 12582928 | tf_op jit(solution)/shard_map/all_gather | solution.py:320
  114.9 6.5 copy.229
  123.9 3.9 slice_bitcast_fusion.4
  134.9 8.7 %fusion = (bf16[2,512,2048]{2,1,0:T(8,128)(2,1)S(1)}, f32[2,512,2048]{2,1,0:T(8,128)}) fusion(f32[2048]{0:T(1024)S(1)} %add.393, bf16[512,1024]{1,0:T(8,128)(2,1)} %get-tuple-element.145, bf16[512,1024]{1,0:T(8,128)(2,1)} %get-tuple-element.146, bf16[2,1,512,512]{2,3,0,1:T(8,128)(2,1)S(1)} %copy.223, f32[512]{0:T(512)S(1)} %add.390, f32[512]{0:T(512)S(1)} %mul.704, ...), kind=kOutput, calls=%fused_computation.9 | convolution fusion | flops 2167406592 | bytes 15749120 | tf_op jit(solution)/shard_map/uth,hf->utf/dot_general | solution.py:258
  155.1 29.3 %attn_fwd.1 = (bf16[2,512,512]{2,1,0:T(8,128)(2,1)}, f32[2,512,512]{2,1,0:T(8,128)}) custom-call(s32[2]{0:T(128)} %copy-done.85, bf16[2,512,512]{2,1,0:T(8,128)(2,1)} %get-tuple-element.158.qu, bf16[2,512,512]{2,1,0:T(8,128)(2,1)} %get-tuple-element.157.qv, bf16[2,512,512]{2,1,0:T(8,128)(2,1)} %fusion.73.k, bf16[2,512,512]{2,1,0:T(8,128)(2,1)} %get-tuple-element.159.v, ...), custom_call_target="tpu_custom_call" | custom-call | tf_op jit(solution)/shard_map/attn_fwd/pallas_call | solution.py:207
  192.5 6.6 multiply_reduce_fusion.20
  199.1 38.9 %psum.21 = f32[3,2,512]{2,1,0:T(2,128)S(1)} all-reduce(f32[3,2,512]{2,1,0:T(2,128)S(1)} %pad_maximum_fusion.7), channel_id=1, replica_groups=mesh['dp'=16,'tensor'=2] {'dp','tensor'}, use_global_device_ids=true, to_apply=%region_9.10 | all-reduce | flops 3072 | bytes 24576 | tf_op jit(solution)/shard_map/psum | solution.py:386
  238.0 3.6 fusion.147
  243.9 3.9 fusion.1
  254.9 3.7 fusion.5
  258.6 6.1 convert_reduce_fusion
  264.7 4.3 fusion.152
  269.1 3.8 fusion.4
  275.8 3.1 multiply_reduce_fusion
  279.3 5.1 convert_reduce_fusion.6
  286.7 3.9 multiply_reduce_fusion.12
  290.6 40.8 %psum.22 = f32[2,2,512]{2,1,0:T(2,128)S(1)} all-reduce(f32[2,2,512]{2,1,0:T(2,128)S(1)} %pad_maximum_fusion.8), channel_id=1, replica_groups=mesh['dp'=16,'tensor'=2] {'dp','tensor'}, use_global_device_ids=true, to_apply=%region_20.21 | all-reduce | flops 2048 | bytes 16384 | tf_op jit(solution)/shard_map/psum | solution.py:422
  331.4 12.4 %multiply_reduce_fusion.3 = (f32[512]{0:T(512)S(1)}, f32[512]{0:T(512)S(1)}, f32[512]{0:T(512)S(1)}, f32[512]{0:T(512)S(1)}, f32[512]{0:T(512)S(1)}, /*index=5*/...) fusion(f32[2,512,512]{1,2,0:T(8,128)} %copy-done.11, ...), kind=kLoop, calls=%fused_computation.112 | loop fusion | flops 14151168 | bytes 8433664 | tf_op jit(solution)/shard_map/reduce_sum | solution.py:97
  343.8 5.4 fusion.71
  354.0 3.2 fusion.151
  369.5 53.6 %attn_bwd.1 = (bf16[2,512,512]{2,1,0:T(8,128)(2,1)}, bf16[2,512,512]{2,1,0:T(8,128)(2,1)}, bf16[2,512,512]{2,1,0:T(8,128)(2,1)}, bf16[2,1024,512]{2,1,0:T(8,128)(2,1)}, f32[2,8,512]{2,1,0:T(8,128)}) custom-call(s32[2]{0:T(128)} %copy-done.85, bf16[2,512,512]{2,1,0:T(8,128)(2,1)} %get-tuple-element.158.qu, bf16[2,512,512]{2,1,0:T(8,128)(2,1)} %get-tuple-element.157.qv, ...), custom_call_target="tpu_custom_call" | custom-call | tf_op jit(solution)/shard_map/attn_bwd/pallas_call | solution.py:226
  423.2 6.2 fusion.150
  429.4 3.2 bitcast_convert_fusion.4
  440.6 3.8 fusion.3
  445.2 5.8 convert_reduce_fusion.1
  451.1 4.3 fusion.149
  455.3 3.9 fusion.2
  499.5 5.0 copy.298
  506.9 3.3 fusion.74
  512.4 96.7 %all-reduce.5.cloned.1.call-done = f32[19968]{0:T(1024)} async-done(((f32[19968]{0:T(1024)}), f32[19968]{0:T(1024)}) %all-reduce.5.cloned.1.call-update) | async-done | bytes 79888 | tf_op jit(solution)/shard_map/psum | solution.py:471
  614.9 158.0 %reduce-scatter.2.cloned.1.call-done = bf16[32,6144]{1,0:T(8,128)(2,1)} async-done(((bf16[1024,6144]{1,0:T(8,128)(2,1)}), bf16[32,6144]{1,0:T(8,128)(2,1)}) %reduce-scatter.2.cloned.1.call-update) | async-done | bytes 393232 | tf_op jit(solution)/shard_map/reduce_scatter | solution.py:469
  (469 shorter events, 151.2 us)
Async XLA Ops:
  7.2 66.2 %copy-start = (s32[2,2]{1,0:T(2,128)S(1)}, s32[2,2]{1,0:T(2,128)}, u32[]{:S(2)}) copy-start(s32[2,2]{1,0:T(2,128)} %param.18) | copy-start | bytes 52
  7.2 107.7 %all-gather.3.cloned.1.call-start = ((), (), s32[]{:S(2)}) async-start(), calls=%async_computation.1 | async-start | bytes 12976128 | tf_op jit(solution)/shard_map/all_gather | solution.py:320
  15.1 594.0 %all-reduce.5.cloned.1.call-start = ((), (), s32[]{:S(2)}) async-start(), calls=%async_computation.3 | async-start | bytes 163840 | tf_op jit(solution)/shard_map/psum | solution.py:471
  63.5 8.0 %copy-start.52 = (bf16[2,1,512,512]{3,2,1,0:T(8,128)(2,1)S(1)}, bf16[2,1,512,512]{3,2,1,0:T(8,128)(2,1)}, u32[]{:S(2)}) copy-start(bf16[2,1,512,512]{3,2,1,0:T(8,128)(2,1)} %param.17) | copy-start | bytes 3145732
  66.2 5.8 copy-start.53
  71.0 75.4 %copy-start.88 = (f32[512]{0:T(512)}, f32[512]{0:T(512)S(1)}, u32[]{:S(2)}) copy-start(f32[512]{0:T(512)S(1)} %add.403) | copy-start | bytes 6148
  71.3 63.5 %copy-start.86 = (f32[512]{0:T(512)}, f32[512]{0:T(512)S(1)}, u32[]{:S(2)}) copy-start(f32[512]{0:T(512)S(1)} %add.390) | copy-start | bytes 6148
  71.4 63.4 %copy-start.77 = (f32[512]{0:T(512)}, f32[512]{0:T(512)S(1)}, u32[]{:S(2)}) copy-start(f32[512]{0:T(512)S(1)} %mul.704) | copy-start | bytes 6148
  73.5 47.9 %copy-start.85 = (s32[2]{0:T(128)}, s32[2]{0:T(128)S(1)}, u32[]{:S(2)}) copy-start(s32[2]{0:T(128)S(1)} %fusion.95.len_ref) | copy-start | bytes 28
  74.0 60.8 %copy-start.72 = (f32[2,512]{1,0:T(2,128)}, f32[2,512]{1,0:T(2,128)S(1)}, u32[]{:S(2)}) copy-start(f32[2,512]{1,0:T(2,128)S(1)} %broadcast_multiply_fusion.14) | copy-start | bytes 12292
  74.4 60.5 %copy-start.74 = (f32[2,512]{1,0:T(2,128)}, f32[2,512]{1,0:T(2,128)S(1)}, u32[]{:S(2)}) copy-start(f32[2,512]{1,0:T(2,128)S(1)} %add_rsqrt_fusion.5) | copy-start | bytes 12292
  134.8 8.7 %copy-start.42 = (bf16[512,1024]{1,0:T(8,128)(2,1)S(1)}, bf16[512,1024]{1,0:T(8,128)(2,1)}, u32[]{:S(2)}) copy-start(bf16[512,1024]{1,0:T(8,128)(2,1)} %get-tuple-element.143) | copy-start | bytes 3145732
  134.8 8.7 %copy-start.44 = (bf16[512,1024]{1,0:T(8,128)(2,1)S(1)}, bf16[512,1024]{1,0:T(8,128)(2,1)}, u32[]{:S(2)}) copy-start(bf16[512,1024]{1,0:T(8,128)(2,1)} %get-tuple-element.144) | copy-start | bytes 3145732
  155.1 29.3 %copy-start.30 = (bf16[512,256]{1,0:T(8,128)(2,1)S(1)}, bf16[512,256]{1,0:T(8,128)(2,1)}, u32[]{:S(2)}) copy-start(bf16[512,256]{1,0:T(8,128)(2,1)} %get-tuple-element.151) | copy-start | bytes 786436
  192.4 6.6 copy-start.11
  192.4 45.6 %copy-start.90 = (f32[512]{0:T(512)S(1)}, f32[512]{0:T(512)}, u32[]{:S(2)}) copy-start(f32[512]{0:T(512)} %add.440) | copy-start | bytes 6148
  192.5 45.5 %copy-start.97 = (f32[512]{0:T(512)S(1)}, f32[512]{0:T(512)}, u32[]{:S(2)}) copy-start(f32[512]{0:T(512)} %add.444) | copy-start | bytes 6148
  241.6 27.5 %copy-start.12 = (f32[2,512,512]{1,2,0:T(8,128)}, f32[2,512,512]{1,2,0:T(8,128)S(1)}, u32[]{:S(2)}) copy-start(f32[2,512,512]{1,2,0:T(8,128)S(1)} %get-tuple-element.235) | copy-start | bytes 6291460
  279.3 5.1 copy-start.18
  331.4 12.4 %copy-start.10 = (f32[2,512,2,512]{1,3,0,2:T(8,128)S(1)}, f32[2,512,2,512]{1,3,0,2:T(8,128)}, u32[]{:S(2)}) copy-start(f32[2,512,2,512]{1,3,0,2:T(8,128)} %copy-done.9) | copy-start | bytes 12582916
  423.1 6.2 copy-start.89
  423.1 6.2 copy-start.100
  423.1 6.2 copy-start.101
  423.2 6.2 copy-start.102
  438.4 6.0 slice-start
  439.9 4.4 copy-start.19
  440.5 4.6 slice-start.1
  445.2 5.8 copy-start.40
  445.2 5.8 copy-start.41
  451.0 4.3 copy-start.73
  490.3 282.6 %reduce-scatter.2.cloned.1.call-start = ((), (), s32[]{:S(2)}) async-start(), calls=%async_computation.2 | async-start | bytes 12976128 | tf_op jit(solution)/shard_map/reduce_scatter | solution.py:469
  510.2 268.6 %copy-start.1 = (s32[2,2]{1,0:T(2,128)S(1)}, s32[2,2]{1,0:T(2,128)}, u32[]{:S(2)}) copy-start(s32[2,2]{1,0:T(2,128)} %param.18) | copy-start | bytes 52
  (78 other events, 171.9 us)
Sparse Core Ops, SparseCore 0:
  15.2 99.5 all-gather.2
  490.4 118.6 all-reduce.4
  615.2 157.6 reduce-scatter.1

commit v2 on v1

--- a/solution.py
+++ b/solution.py
@@ -251,6 +251,279 @@
     )(lens, qu, qv, k, v, pos, o, lse, do)
 
 
+MESH = pl.DeviceIdType.MESH
+NZ, NY, NX = 4, 2, 2
+ANY = pl.BlockSpec(memory_space=pl.ANY)
+VM = pl.BlockSpec(memory_space=pltpu.VMEM)
+
+
+def own_mesh(sizes):
+    return sizes == (NZ * NY * NX, 2)
+
+
+def place():
+    dp = lax.axis_index("dp")
+    return dp // (NY * NX), dp // NX % NY, dp % NX, lax.axis_index("tensor")
+
+
+def dev(z, y, x, t):
+    return (z * (NY * NX) + y * NX + x, t)
+
+
+def greet(peers):
+    barrier = pltpu.get_barrier_semaphore()
+    for peer in peers:
+        pl.semaphore_signal(barrier, inc=1, device_id=peer, device_id_type=MESH)
+    pl.semaphore_wait(barrier, len(peers))
+
+
+def rcopy(src, dst, send, recv, peer):
+    return pltpu.make_async_remote_copy(
+        src_ref=src, dst_ref=dst, send_sem=send, recv_sem=recv, device_id=peer, device_id_type=MESH
+    )
+
+
+def link_peers(z, y, x, t):
+    peers = [dev(lax.rem(z + d, NZ), y, x, t) for d in range(1, NZ)]
+    return peers + [dev(z, 1 - y, x, t), dev(z, y, 1 - x, t), dev(z, y, x, 1 - t)]
+
+
+def sum_kernel(x_ref, o_ref, mid, b1, b2, s1, r1, s2, r2):
+    z, y, x, t = place()
+    spot = (y * NX + x) * 2 + t
+    zs = [dev(lax.rem(z + d, NZ), y, x, t) for d in range(1, NZ)]
+    flat = [lax.rem(spot + d, 8) for d in range(1, 8)]
+    plane = [dev(z, p // 4, p // 2 % 2, p % 2) for p in flat]
+    greet(zs + plane)
+    first = [rcopy(x_ref, b1.at[i], s1.at[i], r1.at[i], peer) for i, peer in enumerate(zs)]
+    for copy in first:
+        copy.start()
+    for copy in first:
+        copy.wait_recv()
+    mid[...] = (x_ref[...] + b1[0]) + (b1[1] + b1[2])
+    second = [rcopy(mid, b2.at[i], s2.at[i], r2.at[i], peer) for i, peer in enumerate(plane)]
+    for copy in second:
+        copy.start()
+    for copy in second:
+        copy.wait_recv()
+    total = mid[...]
+    for i in range(7):
+        total = total + b2[i]
+    o_ref[...] = total
+    for copy in first + second:
+        copy.wait_send()
+
+
+def sum_all(item, cid):
+    return pl.pallas_call(
+        sum_kernel,
+        out_shape=jax.ShapeDtypeStruct(item.shape, F32),
+        in_specs=[VM],
+        out_specs=VM,
+        scratch_shapes=[
+            pltpu.VMEM(item.shape, F32),
+            pltpu.VMEM((3,) + item.shape, F32),
+            pltpu.VMEM((7,) + item.shape, F32),
+            pltpu.SemaphoreType.DMA((3,)),
+            pltpu.SemaphoreType.DMA((3,)),
+            pltpu.SemaphoreType.DMA((7,)),
+            pltpu.SemaphoreType.DMA((7,)),
+        ],
+        compiler_params=pltpu.CompilerParams(collective_id=cid, has_side_effects=True),
+        name="sum_all",
+    )(item)
+
+
+def gather_kernel(widths, x_ref, g_ref, zs, zr, as_, ar, bs, br, cs, cr, own_sem):
+    z, y, x, t = place()
+    greet(link_peers(z, y, x, t))
+    count = len(widths)
+    cols = []
+    at = 0
+    for w in widths:
+        cols.append(pl.ds(at, w))
+        at += w
+    own = pltpu.make_async_copy(x_ref, g_ref.at[t, z, y, x], own_sem)
+    own.start()
+    zc, ac, bc, cc = [], [], [], []
+    for p, c in enumerate(cols):
+        for d in range(1, NZ):
+            zc.append(
+                rcopy(
+                    x_ref.at[:, c],
+                    g_ref.at[t, z, y, x, :, c],
+                    zs.at[p, d - 1],
+                    zr.at[p, d - 1],
+                    dev(lax.rem(z + d, NZ), y, x, t),
+                )
+            )
+            zc[-1].start()
+        along_x, along_y = dev(z, y, 1 - x, t), dev(z, 1 - y, x, t)
+        line = g_ref.at[t, :, y, x, :, c]
+        ac.append(rcopy(line, line, as_.at[p], ar.at[p], along_x if p % 2 == 0 else along_y))
+        half = g_ref.at[t, :, y, :, :, c] if p % 2 == 0 else g_ref.at[t, :, :, x, :, c]
+        bc.append(rcopy(half, half, bs.at[p], br.at[p], along_y if p % 2 == 0 else along_x))
+        full = g_ref.at[t, :, :, :, :, c]
+        cc.append(rcopy(full, full, cs.at[p], cr.at[p], dev(z, y, x, 1 - t)))
+    own.wait()
+    pairs = count // 2
+    for q in range(pairs + 2):
+        for p in (2 * q, 2 * q + 1):
+            if p < count:
+                for d in range(NZ - 1):
+                    zc[p * (NZ - 1) + d].wait_recv()
+                ac[p].start()
+        for p in (2 * q - 2, 2 * q - 1):
+            if 0 <= p < count:
+                ac[p].wait_recv()
+                bc[p].start()
+        for p in (2 * q - 4, 2 * q - 3):
+            if 0 <= p < count:
+                bc[p].wait_recv()
+                cc[p].start()
+    for copy in cc:
+        copy.wait_recv()
+    for copy in zc + ac + bc + cc:
+        copy.wait_send()
+
+
+def gather_all(packed, widths, cid):
+    rows, total = packed.shape
+    n = len(widths)
+    dma = pltpu.SemaphoreType.DMA
+    return pl.pallas_call(
+        lambda *refs: gather_kernel(widths, *refs),
+        out_shape=jax.ShapeDtypeStruct((2, NZ, NY, NX, rows, total), packed.dtype),
+        in_specs=[VM],
+        out_specs=ANY,
+        scratch_shapes=[
+            dma((n, NZ - 1)), dma((n, NZ - 1)), dma((n,)), dma((n,)), dma((n,)), dma((n,)),
+            dma((n,)), dma((n,)), dma,
+        ],
+        compiler_params=pltpu.CompilerParams(collective_id=cid, has_side_effects=True),
+        name="gather_all",
+    )(packed)
+
+
+def scatter_kernel(
+    widths, g_ref, s_ref, o_ref, os_ref, own, rc, ra, rb, rz, sown, src, sra, srb, srz,
+    lsem, cs, cr, as_, ar, bs, br, zs, zr,
+):
+    z, y, x, t = place()
+    along_x, along_y = dev(z, y, 1 - x, t), dev(z, 1 - y, x, t)
+    mate = dev(z, y, x, 1 - t)
+    count = len(widths) + 1
+    bufs = []
+    at = 0
+    for w in widths:
+        c = pl.ds(at, w)
+        cut = (slice(None),) * 4 + (c,)
+        bufs.append(
+            dict(
+                g=lambda i, c=c: g_ref.at[i, :, :, :, :, c],
+                own=own.at[:, :, :, :, c], rc=rc.at[:, :, :, :, c],
+                ra=ra.at[:, :, :, c], rb=rb.at[:, :, c], rz=rz.at[:, :, c], out=o_ref.at[:, c],
+            )
+        )
+        at += w
+    bufs.append(
+        dict(g=lambda i: s_ref.at[i], own=sown, rc=src, ra=sra, rb=srb, rz=srz, out=os_ref)
+    )
+    greet(link_peers(z, y, x, t))
+    lc, cc, ac, bc, zc = [], [], [], [], []
+    for p, b in enumerate(bufs):
+        even = p % 2 == 0
+        lc.append(pltpu.make_async_copy(b["g"](t), b["own"], lsem.at[p]))
+        cc.append(rcopy(b["g"](1 - t), b["rc"], cs.at[p], cr.at[p], mate))
+        away = b["own"].at[:, 1 - y] if even else b["own"].at[:, :, 1 - x]
+        ac.append(rcopy(away, b["ra"], as_.at[p], ar.at[p], along_y if even else along_x))
+        line = b["own"].at[:, y, 1 - x] if even else b["own"].at[:, 1 - y, x]
+        bc.append(rcopy(line, b["rb"], bs.at[p], br.at[p], along_x if even else along_y))
+        for d in range(1, NZ):
+            far = lax.rem(z + d, NZ)
+            zc.append(
+                rcopy(
+                    b["own"].at[far, y, x], b["rz"].at[d - 1], zs.at[p, d - 1], zr.at[p, d - 1],
+                    dev(far, y, x, t),
+                )
+            )
+        lc[p].start()
+        cc[p].start()
+    for q in range(count + 3):
+        if q < count:
+            lc[q].wait()
+            cc[q].wait_recv()
+            b = bufs[q]
+            for i in range(NZ):
+                b["own"][i] = b["own"][i] + b["rc"][i]
+            ac[q].start()
+        p = q - 1
+        if 0 <= p < count:
+            ac[p].wait_recv()
+            b = bufs[p]
+            for i in range(NZ):
+                if p % 2 == 0:
+                    b["own"][i, y] = b["own"][i, y] + b["ra"][i]
+                else:
+                    b["own"][i, :, x] = b["own"][i, :, x] + b["ra"][i]
+            bc[p].start()
+        p = q - 2
+        if 0 <= p < count:
+            bc[p].wait_recv()
+            b = bufs[p]
+            for i in range(NZ):
+                b["own"][i, y, x] = b["own"][i, y, x] + b["rb"][i]
+            for d in range(NZ - 1):
+                zc[p * (NZ - 1) + d].start()
+        p = q - 3
+        if 0 <= p < count:
+            for d in range(NZ - 1):
+                zc[p * (NZ - 1) + d].wait_recv()
+            b = bufs[p]
+            total = b["own"][z, y, x].astype(F32)
+            for d in range(NZ - 1):
+                total = total + b["rz"][d].astype(F32)
+            b["out"][...] = total
+    for copy in cc + ac + bc + zc:
+        copy.wait_send()
+
+
+def scatter_all(grads, small, widths, cid):
+    rows, total = grads.shape[-2:]
+    n = len(widths) + 1
+    dma = pltpu.SemaphoreType.DMA
+    tail = small.shape[-2:]
+
+    def set_of(shape, dtype):
+        return [
+            pltpu.VMEM((NZ, NY, NX) + shape, dtype),
+            pltpu.VMEM((NZ, NY, NX) + shape, dtype),
+            pltpu.VMEM((NZ, 2) + shape, dtype),
+            pltpu.VMEM((NZ,) + shape, dtype),
+            pltpu.VMEM((NZ - 1,) + shape, dtype),
+        ]
+
+    return pl.pallas_call(
+        lambda *refs: scatter_kernel(widths, *refs),
+        out_shape=[
+            jax.ShapeDtypeStruct((rows, total), F32),
+            jax.ShapeDtypeStruct(tail, F32),
+        ],
+        in_specs=[ANY, ANY],
+        out_specs=[VM, VM],
+        scratch_shapes=set_of((rows, total), BF)
+        + set_of(tail, F32)
+        + [
+            dma((n,)), dma((n,)), dma((n,)), dma((n,)), dma((n,)), dma((n,)), dma((n,)),
+            dma((n, NZ - 1)), dma((n, NZ - 1)),
+        ],
+        compiler_params=pltpu.CompilerParams(
+            collective_id=cid, has_side_effects=True, vmem_limit_bytes=56 * 1024 * 1024
+        ),
+        name="scatter_all",
+    )(grads, small)
+
+
 def ffn_forward(residual, gain, shift, out_bias, weights):
     w_in, w_out_t, b_in = weights
     normed, scaled, inv_std = norm_forward(residual, gain, shift)
@@ -274,6 +547,16 @@
     d_hn = jnp.einsum("utf,hf->uth", dz, w_in, preferred_element_type=F32)
     d_x, g_gain, g_shift = norm_backward(d_hn, scaled, inv_std, gain)
     return d_x, (g_in, g_out, g_b), (g_gain, g_shift, g_bias)
+
+
+EXTRA = 256
+
+
+def split_cols(total):
+    tiles = total // 128
+    count = 10
+    base = tiles // count
+    return [128 * (base + (1 if i < tiles - base * count else 0)) for i in range(count)]
 
 
 SEGS = ("f1i", "f1o", "qkv", "pos", "out", "ci", "co", "f2i", "f2o")
@@ -316,16 +599,21 @@
     )
     sizes = [item.shape[1] for item in shards]
     starts = [sum(sizes[:i]) for i in range(len(sizes))]
-    packed = jnp.concatenate(shards, axis=1)
-    every = lax.all_gather(packed, both, axis=0, tiled=True)
-    every = every.reshape(n_dp, 2, rows, -1).transpose(1, 0, 2, 3).reshape(2, n_dp * rows, -1)
+    small_ins = (ffn1_bias, attn_bias, conv_channel, ffn2_bias, norm_params)
+    small = jnp.concatenate([item.reshape(-1) for item in small_ins])
+    extra = jnp.pad(small, (0, rows * EXTRA - small.size)).reshape(rows, EXTRA)
+    packed = jnp.concatenate(shards + (extra,), axis=1)
+    mine_mesh = own_mesh((n_dp, lax.axis_size("tensor"))) and rows % 16 == 0
+    if mine_mesh:
+        every = gather_all(packed, split_cols(packed.shape[1]), 1)
+        every = every.reshape(2, n_dp * rows, -1)
+    else:
+        every = lax.all_gather(packed, both, axis=0, tiled=True)
+        every = every.reshape(n_dp, 2, rows, -1).transpose(1, 0, 2, 3).reshape(2, n_dp * rows, -1)
     full_w = {}
     for name, start, size in zip(SEGS, starts, sizes):
         full_w[name] = (every[0, :, start : start + size], every[1, :, start : start + size])
-    small = jnp.concatenate(
-        [item.reshape(-1) for item in (ffn1_bias, attn_bias, conv_channel, ffn2_bias, norm_params)]
-    )
-    smalls = lax.all_gather(small, both, axis=0, tiled=False).reshape(n_dp, 2, -1).astype(F32)
+    smalls = every[:, :, -EXTRA:].reshape(2, n_dp, -1).transpose(1, 0, 2).astype(F32)
 
     def take(item, offset):
         return smalls[:, :, offset : offset + item.size].reshape((n_dp, 2) + item.shape)
@@ -383,15 +671,21 @@
     def by_micro(item):
         return jnp.sum(item.reshape(micro, seqs, full, width), axis=(1, 2))
 
-    stats = lax.psum(
+    def reduce_sum(item, cid):
+        if mine_mesh:
+            return sum_all(item.reshape(-1, 128), cid).reshape(item.shape)
+        return lax.psum(item, both)
+
+    counts = jnp.sum(lens.reshape(micro, seqs), axis=1).astype(F32)
+    stats = reduce_sum(
         jnp.stack(
             [
                 by_micro(conv * mask3),
                 by_micro(conv * conv * mask3),
-                by_micro(jnp.broadcast_to(mask3, conv.shape)),
+                jnp.broadcast_to(counts[:, None], (micro, width)),
             ]
         ),
-        both,
+        2,
     )
     avg = stats[0] / stats[2]
     var = stats[1] / stats[2] - avg * avg
@@ -419,7 +713,7 @@
     g_scale = jnp.sum(d_bn * yhat, axis=(0, 1))
     g_offset = jnp.sum(d_bn, axis=(0, 1))
     d_yhat = d_bn * cvec[2]
-    sums = lax.psum(jnp.stack([by_micro(d_yhat), by_micro(d_yhat * yhat)]), both)
+    sums = reduce_sum(jnp.stack([by_micro(d_yhat), by_micro(d_yhat * yhat)]), 3)
     d_conv = spread(rstd) * (
         d_yhat - mask3 * (spread(sums[0]) + yhat * spread(sums[1])) / spread(stats[2])
     )
@@ -462,53 +756,63 @@
     wide = (
         grads_f1[0], grads_f1[1], g_qkv, g_pos, g_out, g_ci, g_co, grads_f2[0], grads_f2[1],
     )
+    vecs = (
+        grads_f1[2].reshape(1, -1), g_vec, g_cvec, grads_f2[2].reshape(1, -1),
+    )
+
+    def small_of(item, like):
+        lead = item.shape[0]
+        item = item.reshape(lead, 2, like.shape[-2], n_dp, like.shape[-1])
+        return item.transpose(1, 3, 0, 2, 4).reshape(2, n_dp, -1)
+
+    cols = norm_params.shape[1]
+    small_g = jnp.concatenate(
+        [small_of(item, like) for item, like in zip(vecs, small_ins)]
+        + [
+            g_norm.reshape(-1, n_dp, 2, cols).transpose(2, 1, 0, 3).reshape(2, n_dp, -1),
+        ],
+        axis=2,
+    )
     grads = jnp.stack(
-        [jnp.concatenate([half(item, t) for item in wide], axis=2).astype(BF) for t in (0, 1)],
-        axis=1,
-    ).reshape(n_dp * 2 * rows, -1)
-    own = lax.psum_scatter(grads, both, scatter_dimension=0, tiled=True).astype(F32)
+        [jnp.concatenate([half(item, t) for item in wide], axis=2).astype(BF) for t in (0, 1)]
+    )
+    if mine_mesh:
+        small_g = jnp.pad(small_g, ((0, 0), (0, 0), (0, 1024 - small_g.shape[2])))
+        own, own_small = scatter_all(
+            grads.reshape(2, NZ, NY, NX, rows, -1),
+            small_g.reshape(2, NZ, NY, NX, 8, 128),
+            split_cols(grads.shape[-1]),
+            4,
+        )
+        own_small = own_small.reshape(-1)
+    else:
+        grads = grads.swapaxes(0, 1).reshape(n_dp * 2 * rows, -1)
+        own = lax.psum_scatter(grads, both, scatter_dimension=0, tiled=True).astype(F32)
+        small_g = small_g.swapaxes(0, 1).reshape(n_dp * 2, -1)
+        own_small = lax.psum_scatter(small_g, both, scatter_dimension=0, tiled=True).reshape(-1)
     outs = [own[:, start : start + size] for start, size in zip(starts, sizes)]
-    tiny = lax.psum(
-        jnp.concatenate(
-            [item.reshape(-1) for item in (grads_f1[2], grads_f2[2], g_vec, g_cvec, g_norm)]
-        ),
-        both,
-    )
-    at = lax.axis_index("dp")
-
-    def owned(offset, like, lead):
-        groups = 2 * like.shape[-2]
-        area = tiny[offset : offset + lead * groups * 128].reshape(lead, groups, 128)
-        area = lax.dynamic_slice_in_dim(area, mine * like.shape[-2], like.shape[-2], 1)
-        return lax.dynamic_slice_in_dim(area, at * like.shape[-1], like.shape[-1], 2).reshape(
-            like.shape
-        )
-
-    o1 = 0
-    o2 = grads_f1[2].size
-    o3 = o2 + grads_f2[2].size
-    o4 = o3 + g_vec.size
-    o5 = o4 + g_cvec.size
-    gn = tiny[o5 : o5 + g_norm.size].reshape(g_norm.shape)
-    cols = norm_params.shape[1]
-    gn = lax.dynamic_slice_in_dim(gn, (at * 2 + mine) * cols, cols, 1)
+    small_outs = []
+    off = 0
+    for item in small_ins:
+        small_outs.append(own_small[off : off + item.size].reshape(item.shape))
+        off += item.size
     return (
         result.astype(BF).reshape(frames.shape),
         d0.reshape(frames.shape),
         outs[0],
         outs[1].T,
-        owned(o1, ffn1_bias, 1),
+        small_outs[0],
         outs[2].reshape(qkv_weight.shape),
         outs[3],
         outs[4].T,
-        owned(o3, attn_bias, attn_bias.shape[0]),
+        small_outs[1],
         outs[5].reshape(conv_in.shape),
         outs[6].T,
-        owned(o4, conv_channel, conv_channel.shape[0]),
+        small_outs[2],
         outs[7],
         outs[8].T,
-        owned(o2, ffn2_bias, 1),
-        gn,
+        small_outs[3],
+        small_outs[4],
     )
 
 

time: 793 us -> 620 us (0.78)
  waiting for transfers between devices: 293 us -> 0 us
  Pallas kernels: 82.9 us -> 259 us
  blocking collectives: 123 us -> 0 us
  local copies, waits for them, and re-layouts: 120 us -> 163 us
  other arithmetic: 61.1 us -> 82.5 us
  matrix products: 89.3 us -> 105 us
  between operations: 15.6 us -> 3.09 us
    pallas_call x0 -> x4, Pallas kernels: none -> 176 us  [the longest x1 78.9 us: gather_all(): pl.pallas_call(lambda *refs: gather_kernel(widths, *refs), out_shape=jax....]
    reduce_scatter x1 -> x0, waiting for transfers between devices: 158 us -> none  [local(): lax.psum_scatter(grads, both, scatter_dimension=0, tiled=True).astype(F32)]
    psum x1 -> x0, waiting for transfers between devices: 96.7 us -> none  [local(): lax.psum(jnp.concatenate([item.reshape(-1) for item in (grads_f1[2], grad...]
    psum x2 -> x0, blocking collectives: 79.7 us -> none  [the longest x1 40.8 us: local(): lax.psum(jnp.stack([by_micro(d_yhat), by_micro(d_yhat * yhat)]), both)]
    unnamed x1 -> x0, blocking collectives: 43.2 us -> none
    all_gather x1 -> x0, waiting for transfers between devices: 38.6 us -> none  [local(): every = lax.all_gather(packed, both, axis=0, tiled=True)]
    unnamed x253 -> x339, local copies, waits for them, and re-layouts: 39.6 us -> 48.3 us
  transfers between devices with their start and end apart: 3 -> 0, of which waited for: 3 -> 0; matrix products, arithmetic and copies ran while one was open for 5% -> 0% of each run, Pallas kernels for 0% -> 0%
where the time goes in v2:
time: 620 us; the launch traced here: 612 us
  Pallas kernels  259 us (42%)
  local copies, waits for them, and re-layouts  163 us (26%)
  matrix products  105 us (17%)
  other arithmetic  82.5 us (13%)
    pallas_call x1, Pallas kernels, gather_all(): pl.pallas_call(lambda *refs: gather_kernel(widths, *refs), out_shape=jax....  78.9 us
    pallas_call x1, Pallas kernels, scatter_all(): pl.pallas_call(lambda *refs: scatter_kernel(widths, *refs), out_shape=[ja...  74.2 us
    pallas_call x1, Pallas kernels, attn_bwd_call(): pl.pallas_call(attn_bwd_kernel, grid_spec=pltpu.PrefetchScalarGridSpec(nu...  53.7 us
    unnamed x339, local copies, waits for them, and re-layouts  48.3 us
    pallas_call x1, Pallas kernels, attn_fwd_call(): pl.pallas_call(attn_fwd_kernel, grid_spec=pltpu.PrefetchScalarGridSpec(nu...  29.1 us
    pallas_call x2, Pallas kernels, sum_all(): pl.pallas_call(sum_kernel, out_shape=jax.ShapeDtypeStruct(item.shape, F32...  22.8 us
    dot_general x2, matrix products, ffn_forward(): zf = jnp.einsum('uth,hf->utf', hn, w_in, preferred_element_type=F32) + b_in  17.6 us
    dot_general x2, matrix products, ffn_backward(): d_af = jnp.einsum('uth,hf->utf', g, w_out_t, preferred_element_type=F32)  16.8 us

profile of v2, /device:TPU:0, one launch (start us, length us, event | category | flops | bytes accessed | tf_op | source)
XLA Modules:
  0.0 611.9 jit_solution(9013472321719964245)
XLA Ops:
  12.6 78.9 %gather_all.1 = bf16[2,4,2,2,32,6400]{5,4,3,2,1,0:T(8,128)(2,1)} custom-call(bf16[32,6400]{1,0:T(8,128)(2,1)} %copy-done.55), custom_call_target="tpu_custom_call" | custom-call | tf_op jit(solution)/shard_map/gather_all/pallas_call | solution.py:394
  92.9 4.7 copy.80
  100.9 5.9 slice_bitcast_fusion.4
  108.9 7.1 %fusion = (bf16[2,512,2048]{2,1,0:T(8,128)(2,1)}, f32[2,512,2048]{2,1,0:T(8,128)}) fusion(f32[2048]{0:T(1024)S(1)} %add.357, bf16[512,1024]{1,0:T(8,128)(2,1)S(1)} %get-tuple-element.117, bf16[512,1024]{1,0:T(8,128)(2,1)S(1)} %get-tuple-element.118, bf16[2,1,512,512]{2,3,0,1:T(8,128)(2,1)S(1)} %copy.77, f32[512]{0:T(512)S(1)} %add.354, f32[512]{0:T(512)S(1)} %mul.684, ...), kind=kOutput, calls=%fused_computation.9 | convolution fusion | flops 2167406592 | bytes 15749120 | tf_op jit(solution)/shard_map/uth,hf->utf/dot_general | solution.py:531
  116.2 5.3 fusion.141
  133.9 6.0 fusion.75
  140.6 4.3 add_convert_fusion.3
  153.6 29.1 %attn_fwd.1 = (bf16[2,512,512]{2,1,0:T(8,128)(2,1)}, f32[2,512,512]{2,1,0:T(8,128)}) custom-call(s32[2]{0:T(128)} %dynamic-slice_reduce_fusion.len_ref, bf16[2,512,512]{2,1,0:T(8,128)(2,1)} %get-tuple-element.133.qu, bf16[2,512,512]{2,1,0:T(8,128)(2,1)} %get-tuple-element.132.qv, bf16[2,512,512]{2,1,0:T(8,128)(2,1)} %fusion.73.k, ...), custom_call_target="tpu_custom_call" | custom-call | tf_op jit(solution)/shard_map/attn_fwd/pallas_call | solution.py:207
  197.9 3.3 convolution_add_fusion
  211.9 12.6 %multiply_reduce_fusion.20 = (f32[2,512]{1,0:T(2,128)S(1)}, f32[2,512]{1,0:T(2,128)S(1)}, f32[2,512,512]{1,2,0:T(8,128)}) fusion(f32[2,512]{1,0:T(2,128)S(1)} %compare_convert_fusion, f32[512]{0:T(512)S(1)} %mul.744, f32[512]{0:T(512)S(1)} %mul.741, f32[512]{0:T(512)S(1)} %mul.738, f32[512]{0:T(512)S(1)} %mul.735, f32[2,512,512]{1,2,0:T(8,128)} %multiply_multiply_fusion, ...), kind=kLoop, calls=%fused_computation.145 | loop fusion | flops 11532288 | bytes 4225024 | tf_op jit(solution)/shard_map/reduce_sum | solution.py:672
  225.3 12.9 %sum_all.2 = f32[24,128]{1,0:T(8,128)} custom-call(f32[24,128]{1,0:T(8,128)} %reshape.1019.x_ref), custom_call_target="tpu_custom_call" | custom-call | tf_op jit(solution)/shard_map/sum_all/pallas_call | solution.py:318
  240.0 3.6 fusion.143
  248.8 10.5 %fusion.1 = (bf16[2,512,2048]{2,1,0:T(8,128)(2,1)}, f32[2,512,2048]{2,1,0:T(8,128)}) fusion(f32[2048]{0:T(1024)} %add.416, bf16[512,1024]{1,0:T(8,128)(2,1)} %get-tuple-element.113, bf16[512,1024]{1,0:T(8,128)(2,1)} %get-tuple-element.114, f32[2,512,512]{1,2,0:T(8,128)} %copy-done.13, f32[512]{0:T(512)} %add.413, f32[512]{0:T(512)} %mul.760, ...), kind=kOutput, calls=%fused_computation.10 | convolution fusion | flops 2166882304 | bytes 16797696 | tf_op jit(solution)/shard_map/uth,hf->utf/dot_general | solution.py:531
  259.4 5.9 fusion.144
  273.8 8.4 %convert_reduce_fusion = (f32[2048]{0:T(1024)}, bf16[2,512,2048]{2,1,0:T(8,128)(2,1)S(1)}) fusion(f32[2,512,2048]{2,1,0:T(8,128)} %get-tuple-element.212, f32[2048]{0:T(1024)S(1)} %copy-done.119, bf16[2,512,512]{1,2,0:T(8,128)(2,1)S(1)} %get-tuple-element.98, bf16[512,1024]{1,0:T(8,128)(2,1)S(1)} %copy-done.45, bf16[512,1024]{1,0:T(8,128)(2,1)S(1)} %copy-done.44), kind=kOutput, calls=%fused_computation.1 | convolution fusion | flops 2176841728 | bytes 15745024 | tf_op jit(solution)/shard_map/uth,hf->utf/dot_general | solution.py:543
  282.2 4.3 fusion.148
  292.7 5.1 convert_reduce_fusion.6
  297.8 4.0 multiply_reduce_fusion.12
  302.4 9.9 %sum_all.3 = f32[16,128]{1,0:T(8,128)} custom-call(f32[16,128]{1,0:T(8,128)} %reshape.1022.x_ref), custom_call_target="tpu_custom_call" | custom-call | tf_op jit(solution)/shard_map/sum_all/pallas_call | solution.py:318
  313.1 13.2 %multiply_reduce_fusion.3 = (f32[512]{0:T(512)}, f32[512]{0:T(512)}, f32[512]{0:T(512)}, f32[512]{0:T(512)}, f32[512]{0:T(512)}, /*index=5*/f32[512]{0:T(512)}, ...) fusion(f32[2,512,512]{1,2,0:T(8,128)} %multiply_multiply_fusion, f32[2,512]{1,0:T(2,128)S(1)} %copy-done.76, ...), kind=kLoop, calls=%fused_computation.112 | loop fusion | flops 14151168 | bytes 8433664 | tf_op jit(solution)/shard_map/reduce_sum | solution.py:97
  326.4 5.6 fusion.71
  339.2 3.1 multiply_reduce_fusion.1
  348.4 53.7 %attn_bwd.1 = (bf16[2,512,512]{2,1,0:T(8,128)(2,1)}, bf16[2,512,512]{2,1,0:T(8,128)(2,1)}, bf16[2,512,512]{2,1,0:T(8,128)(2,1)}, bf16[2,1024,512]{2,1,0:T(8,128)(2,1)}, f32[2,8,512]{2,1,0:T(8,128)}) custom-call(s32[2]{0:T(128)} %dynamic-slice_reduce_fusion.len_ref, bf16[2,512,512]{2,1,0:T(8,128)(2,1)} %get-tuple-element.133.qu, ...), custom_call_target="tpu_custom_call" | custom-call | tf_op jit(solution)/shard_map/attn_bwd/pallas_call | solution.py:226
  402.1 5.5 fusion.146
  414.9 8.4 %convert_reduce_fusion.1 = (f32[2048]{0:T(1024)}, bf16[2,512,2048]{2,1,0:T(8,128)(2,1)S(1)}) fusion(f32[2,512,2048]{2,1,0:T(8,128)} %get-tuple-element.204, f32[2048]{0:T(1024)S(1)} %copy-done.117, bf16[512,1024]{1,0:T(8,128)(2,1)S(1)} %copy-done.40, bf16[512,1024]{1,0:T(8,128)(2,1)S(1)} %copy-done.41, f32[2,512,512]{1,2,0:T(8,128)S(1)} %get-tuple-element.104), kind=kOutput, calls=%fused_computation.2 | convolution fusion | flops 2177890304 | bytes 16793600 | tf_op jit(solution)/shard_map/uth,hf->utf/dot_general | solution.py:543
  423.4 3.7 fusion.145
  427.1 3.0 copy.142
  454.2 5.2 fusion.3
  487.9 3.3 fusion.65
  511.2 8.6 %pad_maximum_fusion.refs_0_ = bf16[2,4,2,2,32,6144]{5,4,3,2,1,0:T(8,128)(2,1)} fusion(bf16[1,4,2,2,32,6144]{5,4,3,2,1,0:T(8,128)(2,1)S(1)} %constant_dynamic-update-slice_fusion.19, bf16[1,4,2,2,32,6144]{5,4,3,2,1,0:T(8,128)(2,1)} %constant_dynamic-update-slice_fusion.10), kind=kLoop, calls=%fused_computation | loop fusion | flops 6291456 | bytes 25165824 | tf_op jit(solution)/shard_map/stack | solution.py:776
  519.8 74.2 %scatter_all.1 = (f32[32,6144]{1,0:T(8,128)}, f32[8,128]{1,0:T(8,128)}) custom-call(bf16[2,4,2,2,32,6144]{5,4,3,2,1,0:T(8,128)(2,1)} %pad_maximum_fusion.refs_0_, f32[2,4,2,2,8,128]{5,4,3,2,1,0:T(8,128)} %bitcast.409), custom_call_target="tpu_custom_call" | custom-call | tf_op jit(solution)/shard_map/scatter_all/pallas_call | solution.py:506
  604.7 3.3 fusion.74
  (584 shorter events, 196.3 us)
Async XLA Ops:
  0.6 152.3 %copy-start = (s32[2,2]{1,0:T(2,128)S(1)}, s32[2,2]{1,0:T(2,128)}, u32[]{:S(2)}) copy-start(s32[2,2]{1,0:T(2,128)} %param.18) | copy-start | bytes 52
  121.7 12.1 %copy-start.70 = (f32[2,512]{1,0:T(2,128)}, f32[2,512]{1,0:T(2,128)S(1)}, u32[]{:S(2)}) copy-start(f32[2,512]{1,0:T(2,128)S(1)} %add_rsqrt_fusion.4) | copy-start | bytes 12292
  121.9 12.0 %copy-start.83 = (f32[512]{0:T(512)}, f32[512]{0:T(512)S(1)}, u32[]{:S(2)}) copy-start(f32[512]{0:T(512)S(1)} %mul.692) | copy-start | bytes 6148
  122.0 11.9 %copy-start.124 = (f32[512]{0:T(512)}, f32[512]{0:T(512)S(1)}, u32[]{:S(2)}) copy-start(f32[512]{0:T(512)S(1)} %add.367) | copy-start | bytes 6148
  186.5 11.3 %copy-start.72 = (f32[2,512]{1,0:T(2,128)}, f32[2,512]{1,0:T(2,128)S(1)}, u32[]{:S(2)}) copy-start(f32[2,512]{1,0:T(2,128)S(1)} %add_rsqrt_fusion.3) | copy-start | bytes 12292
  186.6 11.2 %copy-start.85 = (f32[512]{0:T(512)}, f32[512]{0:T(512)S(1)}, u32[]{:S(2)}) copy-start(f32[512]{0:T(512)S(1)} %mul.716) | copy-start | bytes 6148
  186.7 11.1 %copy-start.126 = (f32[512]{0:T(512)}, f32[512]{0:T(512)S(1)}, u32[]{:S(2)}) copy-start(f32[512]{0:T(512)S(1)} %add.388) | copy-start | bytes 6148
  205.4 19.2 %copy-start.88 = (f32[512]{0:T(512)}, f32[512]{0:T(512)S(1)}, u32[]{:S(2)}) copy-start(f32[512]{0:T(512)S(1)} %mul.711) | copy-start | bytes 6148
  211.4 13.2 %copy-start.94 = (f32[512]{0:T(512)}, f32[512]{0:T(512)S(1)}, u32[]{:S(2)}) copy-start(f32[512]{0:T(512)S(1)} %mul.735) | copy-start | bytes 6148
  211.6 13.0 %copy-start.96 = (f32[512]{0:T(512)}, f32[512]{0:T(512)S(1)}, u32[]{:S(2)}) copy-start(f32[512]{0:T(512)S(1)} %mul.738) | copy-start | bytes 6148
  211.7 12.8 %copy-start.98 = (f32[512]{0:T(512)}, f32[512]{0:T(512)S(1)}, u32[]{:S(2)}) copy-start(f32[512]{0:T(512)S(1)} %mul.741) | copy-start | bytes 6148
  211.9 12.7 %copy-start.100 = (f32[512]{0:T(512)}, f32[512]{0:T(512)S(1)}, u32[]{:S(2)}) copy-start(f32[512]{0:T(512)S(1)} %mul.744) | copy-start | bytes 6148
  211.9 12.7 %copy-start.121 = (s32[2]{0:T(128)S(1)}, s32[2]{0:T(128)}, u32[]{:S(2)}) copy-start(s32[2]{0:T(128)} %dynamic-slice_reduce_fusion.len_ref) | copy-start | bytes 28
  211.9 27.8 %copy-start.67 = (f32[1,16,2,16]{3,0,1,2:T(1,128)S(1)}, f32[1,16,2,16]{3,0,1,2:T(1,128)}, u32[]{:S(2)}) copy-start(f32[1,16,2,16]{3,0,1,2:T(1,128)} %get-tuple-element.166) | copy-start | bytes 6148
  297.8 15.2 %copy-start.76 = (f32[2,512]{1,0:T(2,128)S(1)}, f32[2,512]{1,0:T(2,128)}, u32[]{:S(2)}) copy-start(f32[2,512]{1,0:T(2,128)} %copy-done.75) | copy-start | bytes 12292
  313.0 13.3 %copy-start.11 = (f32[2,512,2,512]{1,3,0,2:T(8,128)S(1)}, f32[2,512,2,512]{1,3,0,2:T(8,128)}, u32[]{:S(2)}) copy-start(f32[2,512,2,512]{1,3,0,2:T(8,128)} %copy-done.10) | copy-start | bytes 12582916
  313.0 13.3 %copy-start.89 = (f32[512]{0:T(512)S(1)}, f32[512]{0:T(512)}, u32[]{:S(2)}) copy-start(f32[512]{0:T(512)} %copy-done.88) | copy-start | bytes 6148
  313.0 13.3 %copy-start.90 = (f32[512]{0:T(512)S(1)}, f32[512]{0:T(512)}, u32[]{:S(2)}) copy-start(f32[512]{0:T(512)} %mul.723) | copy-start | bytes 6148
  313.1 13.3 %copy-start.91 = (f32[512]{0:T(512)S(1)}, f32[512]{0:T(512)}, u32[]{:S(2)}) copy-start(f32[512]{0:T(512)} %mul.726) | copy-start | bytes 6148
  313.1 13.3 %copy-start.92 = (f32[512]{0:T(512)S(1)}, f32[512]{0:T(512)}, u32[]{:S(2)}) copy-start(f32[512]{0:T(512)} %mul.729) | copy-start | bytes 6148
  313.1 13.3 %copy-start.93 = (f32[512]{0:T(512)S(1)}, f32[512]{0:T(512)}, u32[]{:S(2)}) copy-start(f32[512]{0:T(512)} %mul.732) | copy-start | bytes 6148
  313.1 13.3 %copy-start.95 = (f32[512]{0:T(512)S(1)}, f32[512]{0:T(512)}, u32[]{:S(2)}) copy-start(f32[512]{0:T(512)} %copy-done.94) | copy-start | bytes 6148
  313.1 13.3 %copy-start.97 = (f32[512]{0:T(512)S(1)}, f32[512]{0:T(512)}, u32[]{:S(2)}) copy-start(f32[512]{0:T(512)} %copy-done.96) | copy-start | bytes 6148
  313.1 13.3 %copy-start.99 = (f32[512]{0:T(512)S(1)}, f32[512]{0:T(512)}, u32[]{:S(2)}) copy-start(f32[512]{0:T(512)} %copy-done.98) | copy-start | bytes 6148
  313.1 13.3 %copy-start.101 = (f32[512]{0:T(512)S(1)}, f32[512]{0:T(512)}, u32[]{:S(2)}) copy-start(f32[512]{0:T(512)} %copy-done.100) | copy-start | bytes 6148
  433.0 13.9 %copy-start.115 = (f32[512]{0:T(512)S(1)}, f32[512]{0:T(512)}, u32[]{:S(2)}) copy-start(f32[512]{0:T(512)} %get-tuple-element.78) | copy-start | bytes 6148
  433.3 14.4 %copy-start.114 = (f32[512]{0:T(512)S(1)}, f32[512]{0:T(512)}, u32[]{:S(2)}) copy-start(f32[512]{0:T(512)} %get-tuple-element.77) | copy-start | bytes 6148
  433.5 14.9 %copy-start.113 = (f32[512]{0:T(512)S(1)}, f32[512]{0:T(512)}, u32[]{:S(2)}) copy-start(f32[512]{0:T(512)} %get-tuple-element.76) | copy-start | bytes 6148
  433.7 15.4 %copy-start.112 = (f32[512]{0:T(512)S(1)}, f32[512]{0:T(512)}, u32[]{:S(2)}) copy-start(f32[512]{0:T(512)} %get-tuple-element.75) | copy-start | bytes 6148
  433.9 15.9 %copy-start.111 = (f32[512]{0:T(512)S(1)}, f32[512]{0:T(512)}, u32[]{:S(2)}) copy-start(f32[512]{0:T(512)} %get-tuple-element.74) | copy-start | bytes 6148
  436.0 15.8 %copy-start.118 = (f32[2048]{0:T(1024)S(1)}, f32[2048]{0:T(1024)}, u32[]{:S(2)}) copy-start(f32[2048]{0:T(1024)} %get-tuple-element.216) | copy-start | bytes 24580
  436.0 16.1 %copy-start.80 = (f32[2,8,512]{2,1,0:T(8,128)S(1)}, f32[2,8,512]{2,1,0:T(8,128)}, u32[]{:S(2)}) copy-start(f32[2,8,512]{2,1,0:T(8,128)} %get-tuple-element.31) | copy-start | bytes 98308
  (109 other events, 411.6 us)
